TPU v7x, 32 devices: a whole 2x2x4 slice. The times are simulated.
32 devices in a mesh: slab: 2 (over x), ang: 16 (over z, y, core).
Axes of the slice: x: 2, y: 2, z: 4, core: 2. Of those that a mesh axis runs over, the one named last changes fastest.
Arguments:
- raw_counts: float32 [4096, 8, 2048], P('ang', 'slab'), parts along dimension 1, may hold values from 500 to 8000
- dark_frames: float32 [4, 8, 2048], P(None, 'slab'), parts along dimension 1, may hold values from 100 to 400
- flat_frames: float32 [8, 8, 2048], P(None, 'slab'), parts along dimension 1, may hold values from 8000 to 12000
- dark_index: int32 [4096], P('ang'), may hold values from 0 to 3
- flat_index: int32 [4096], P('ang'), may hold values from 0 to 7
- center_offset: int32 [1], replicated, may hold values from 64 to 255
- blend_width: int32 [1], replicated, may hold values from 2 to 128
- stripe_gain: float32 [1025], replicated, may hold values from 0.25 to 1
- ramp_window: float32 [2049], replicated, may hold values from 0.5 to 2
Outputs:
- filtered: float32 [2048, 8, 4096], P('ang', 'slab'), parts along dimension 1
There are 2 independent parts, one for each index of `slab`. A program takes and returns all parts, laid end to end along the dimension named above; an argument that names none is the same for every part. Nothing has to cross between parts.
Inputs may be any that keep to these rules, and one draw needn't show every extreme that they name: `blend_width`: the blend width never exceeds twice the center offset.
All inputs are finite; a program needn't handle non-finite values.
Results may differ from a plain program's by a relative error of at most 0.00075.
Values sent between devices are 32-bit elements; how exact they have to be, the bound alone decides.
No kernel may reach another device: no remote copies, remote signals or barrier semaphores. Data moves between devices by JAX's collectives and lax.ppermute only.
A program may use at most 256 MiB of HBM per device.

v0:
```python
import functools

import jax
import jax.numpy as jnp
import numpy as np
from jax import lax
from jax.experimental import pallas as pl
from jax.experimental.pallas import tpu as pltpu
from jax.sharding import PartitionSpec as P

DET = 2048
VIEWS = 2048
STITCH = 2 * DET
EDGE = 64
TILE = 256
CHUNKS = 2
STEP = 128
UNROLL = 4
STRIPE_UNROLL = 2
RAMP_UNROLL = 4
MIB = 1024 * 1024
RAMP_VMEM = 48 * MIB
STRIPE_VMEM = 48 * MIB
PREPARE_VMEM = 56 * MIB

precise = lax.Precision.HIGHEST


def impulse(gains, length):
    inner = 64
    period = length // inner
    outer = period // 2
    phase = lambda rows, cols, whole: 2.0 * np.pi * (np.outer(rows, cols) % whole) / whole
    first = phase(np.arange(period), np.arange(outer), period)
    turn = phase(np.arange(period), np.arange(inner), length)
    last = phase(np.arange(inner), np.arange(inner), inner)
    table = lambda values: jnp.asarray(values.astype(np.float32))
    doubled = np.full((length // 2,), 2.0 / length, np.float32)
    doubled[0] = 1.0 / length
    coefs = (gains[:-1] * doubled).reshape(outer, inner)
    real = jnp.dot(table(np.cos(first)), coefs, precision=precise)
    imag = jnp.dot(table(np.sin(first)), coefs, precision=precise)
    cos_turn, sin_turn = table(np.cos(turn)), table(np.sin(turn))
    turned_real = real * cos_turn - imag * sin_turn
    turned_imag = real * sin_turn + imag * cos_turn
    contract = (((1,), (1,)), ((), ()))
    line = lax.dot_general(table(np.cos(last)), turned_real, contract, precision=precise)
    line = line - lax.dot_general(table(np.sin(last)), turned_imag, contract, precision=precise)
    signs = table(np.where(np.arange(period) % 2 == 0, 1.0, -1.0) / length)
    return (line + signs[None, :] * gains[-1]).reshape(length)


def ring_lines(line):
    quarter = line.shape[0] // 4
    q = line.reshape(4, quarter)
    even, odd = q[0] + q[2], q[1] + q[3]
    cyclic = 0.25 * (even + odd)
    negative = 0.25 * (even - odd)
    wide = 0.5 * jnp.concatenate([q[0] - q[2], q[1] - q[3]])
    return jnp.concatenate([cyclic, cyclic, negative, -negative, wide, -wide])[None, :]


def ring_spans(quarter):
    return ((0, quarter), (2 * quarter, quarter), (4 * quarter, 2 * quarter))


def band_kernel(line_ref, high_ref, low_ref, *, flip):
    quarter = line_ref.shape[1] // 8
    step = TILE if flip else 32
    for start, size in ring_spans(quarter):
        row = line_ref[:, start : start + 2 * size]
        wide = jnp.broadcast_to(row, (step, 2 * size))
        for top in range(0, TILE, step):
            shifted = pltpu.roll(wide, size - TILE + top, 1, stride=1, stride_axis=0)
            if flip:
                shifted = shifted.T
            high = shifted.astype(jnp.bfloat16)
            low = (shifted - high.astype(jnp.float32)).astype(jnp.bfloat16)
            if flip:
                place = (slice(start, start + 2 * size), slice(None))
            else:
                place = (slice(top, top + step), slice(start, start + 2 * size))
            high_ref[place] = high
            low_ref[place] = low


def bands(line, flip):
    size = line.shape[1]
    shape = jax.ShapeDtypeStruct((size, TILE) if flip else (TILE, size), jnp.bfloat16)
    return pl.pallas_call(
        functools.partial(band_kernel, flip=flip),
        out_shape=(shape, shape),
        compiler_params=pltpu.CompilerParams(vmem_limit_bytes=40 * MIB),
        cost_estimate=pl.CostEstimate(
            flops=4 * TILE * size, bytes_accessed=4 * TILE * size, transcendentals=0
        ),
        name="bands",
    )(line)


def split(values):
    high = values.astype(jnp.bfloat16)
    return high, (values - high.astype(jnp.float32)).astype(jnp.bfloat16)


def dot32(left, right, contract):
    return lax.dot_general(left, right, (contract, ((), ())), preferred_element_type=jnp.float32)


def prepare_kernel(
    scalars, dark_index, flat_index, raw_ref, dark_ref, flat_ref, weight_ref, out_ref, turned_ref, *, start
):
    count, rows, share, width = out_ref.shape
    blocks = DET // 128
    lines = dark_ref.shape[1]
    total = lines // blocks
    group = 8 // total if total < 8 else 1
    upper, shift = scalars[0], scalars[1]
    turn, jump = shift % 128, shift // 128
    lane = lax.broadcasted_iota(jnp.int32, (share, 128), 1)
    back = (lane + (128 - turn)) & 127
    pick = jnp.where(upper != 0, 127 - back, back)
    first = pl.program_id(0) * share

    def logs(eight, carry):
        pieces = []
        for one in range(8):
            view = eight * 8 + one
            dark = dark_ref[dark_index[first + view]]
            flat = flat_ref[flat_index[first + view]]
            raw = raw_ref[pl.ds(pl.multiple_of(view * lines, 8), lines), :]
            pieces.append(jnp.log(flat - dark) - jnp.log(raw - dark))
        top = pl.ds(pl.multiple_of(eight * 8, 8), 8)
        stacked = jnp.stack(pieces)
        for part in range(blocks // group):
            square = stacked[:, part * group * total : (part + 1) * group * total]
            square = pltpu.einshape("abc->bac", square)
            for inner in range(group):
                for row in range(rows):
                    turned_ref[row, part * group + inner, top, :] = square[inner * total + start + row]
        return carry

    lax.fori_loop(0, share // 8, logs, 0)

    def turned(block):
        source = jnp.where(upper != 0, blocks - 1 - block, block)
        return [jnp.take_along_axis(turned_ref[row, source], pick, axis=1) for row in range(rows)]

    def body(block, before):
        now = turned(block)
        target = (block + jump) % blocks
        place = pl.ds(pl.multiple_of(target * 128, 128), 128)
        weight = weight_ref[:, place]
        for row in range(rows):
            mixed = jnp.where(lane >= turn, now[row], before[row]) * weight
            if width >= 128:
                per = width // 128
                inside = pl.ds(pl.multiple_of((target % per) * 128, 128), 128)
                out_ref[target // per, row, :, inside] = mixed
            else:
                per = 128 // width
                for part in range(per):
                    out_ref[target * per + part, row] = mixed[:, part * width : (part + 1) * width]
        return now

    lax.fori_loop(0, blocks, body, turned(blocks - 1), unroll=UNROLL)


def prepare(scalars, indices, raw, dark, flat, weight, start, rows, count):
    share = indices[0].shape[0]
    width = DET // count
    step = min(share, STEP)
    lines = raw.shape[0] // share
    return pl.pallas_call(
        functools.partial(prepare_kernel, start=start),
        out_shape=jax.ShapeDtypeStruct((count, rows, share, width), jnp.float32),
        grid_spec=pltpu.PrefetchScalarGridSpec(
            num_scalar_prefetch=3,
            grid=(share // step,),
            in_specs=[
                pl.BlockSpec((lines * step, 128), lambda p, *s: (p, 0)),
                pl.BlockSpec(dark.shape, lambda p, *s: (0, 0, 0)),
                pl.BlockSpec(flat.shape, lambda p, *s: (0, 0, 0)),
                pl.BlockSpec((1, DET), lambda p, *s: (0, 0)),
            ],
            out_specs=pl.BlockSpec((count, rows, step, width), lambda p, *s: (0, 0, p, 0)),
            scratch_shapes=[pltpu.VMEM((rows, DET // 128, step, 128), jnp.float32)],
        ),
        compiler_params=pltpu.CompilerParams(vmem_limit_bytes=PREPARE_VMEM),
        cost_estimate=pl.CostEstimate(
            flops=20 * rows * share * DET,
            bytes_accessed=4 * rows * share * DET + 4 * raw.size,
            transcendentals=2 * raw.size,
        ),
        name="prepare",
    )(scalars, *indices, raw, dark, flat, weight)


def band_place(start, size, block):
    return pl.ds(pl.multiple_of(start + size - TILE - TILE * block, TILE), size)


def destripe_kernel(x_ref, high_ref, low_ref, y_ref, full_ref):
    width = x_ref.shape[3]
    quarter = VIEWS // 4
    x = x_ref[...].reshape(4, quarter, width)
    even, odd = x[0] + x[2], x[1] + x[3]
    wide = jnp.concatenate([x[0] - x[2], x[1] - x[3]], axis=0)
    rings = [split(ring) for ring in (even + odd, even - odd, wide)]
    spans = ring_spans(quarter)

    def product(ring, block):
        place = band_place(*spans[ring], block)
        high, low = high_ref[:, place], low_ref[:, place]
        ring_high, ring_low = rings[ring]
        piece = dot32(high, ring_high, ((1,), (0,)))
        piece += dot32(high, ring_low, ((1,), (0,)))
        return piece + dot32(low, ring_high, ((1,), (0,)))

    count = quarter // TILE

    def body(block, carry):
        cyclic, negative = product(0, block), product(1, block)
        for part, both in enumerate((cyclic + negative, cyclic - negative)):
            wide = product(2, block + part * count)
            top = pl.multiple_of(part * quarter + block * TILE, TILE)
            full_ref[pl.ds(top, TILE), :] = both + wide
            full_ref[pl.ds(top + 2 * quarter, TILE), :] = both - wide
        return carry

    lax.fori_loop(0, count, body, 0, unroll=STRIPE_UNROLL)
    y_ref[...] = full_ref[...].reshape(y_ref.shape)


def destripe(x, high, low, devices):
    count, rows, share, width = x.shape
    views = VIEWS // devices
    band = pl.BlockSpec(high.shape, lambda r: (0, 0), pipeline_mode=pl.Buffered(1))
    return pl.pallas_call(
        destripe_kernel,
        out_shape=jax.ShapeDtypeStruct((devices, rows, views, width), jnp.float32),
        grid=(rows,),
        in_specs=[pl.BlockSpec((count, 1, share, width), lambda r: (0, r, 0, 0)), band, band],
        out_specs=pl.BlockSpec((devices, 1, views, width), lambda r: (0, r, 0, 0)),
        scratch_shapes=[pltpu.VMEM((VIEWS, width), jnp.float32)],
        compiler_params=pltpu.CompilerParams(vmem_limit_bytes=STRIPE_VMEM),
        cost_estimate=pl.CostEstimate(
            flops=3 * 2 * rows * width * VIEWS * 768,
            bytes_accessed=8 * rows * VIEWS * width + 4 * high.size,
            transcendentals=0,
        ),
        name="destripe",
    )(x, high, low)


def ramp_kernel(x_ref, high_ref, low_ref, *refs, total):
    *done_refs, y_ref = refs
    blocks, rows, views, width = x_ref.shape
    half = blocks // 2
    depth = rows * views
    pieces = [x_ref[block].reshape(depth, width) for block in range(blocks)]
    direct = jnp.concatenate(pieces[:half], axis=1)
    partner = jnp.concatenate(pieces[half:], axis=1)
    place = lax.broadcasted_iota(jnp.int32, (1, DET), 1)
    direct_sign = jnp.where(place >= DET - EDGE, 1.0, -1.0)
    partner_sign = jnp.where(place < EDGE, -1.0, 1.0)
    added = direct + partner
    wide = direct * direct_sign + partner * partner_sign
    quarter = DET // 2
    left_half, right_half = added[:, :quarter], added[:, quarter:]
    rings = [split(ring) for ring in (left_half + right_half, left_half - right_half, wide)]
    spans = ring_spans(quarter)

    def product(ring, block):
        place = band_place(*spans[ring], block)
        high, low = high_ref[place, :], low_ref[place, :]
        ring_high, ring_low = rings[ring]
        piece = dot32(ring_high, high, ((1,), (0,)))
        piece += dot32(ring_low, high, ((1,), (0,)))
        return piece + dot32(ring_high, low, ((1,), (0,)))

    def emit(left, values):
        place = pl.ds(pl.multiple_of(left, TILE), TILE)
        values = values.reshape(rows, views, TILE)
        if not total:
            y_ref[:, :, place] = values
            return
        lines = [ref[row, :, place] for ref in done_refs for row in range(ref.shape[0])]
        lines += [values[row] for row in range(rows)]
        parts = TILE // 128
        square = jnp.stack([line[:, part * 128 : (part + 1) * 128] for part in range(parts) for line in lines])
        place = pl.ds(pl.multiple_of(left // 128 * total, parts * total), parts * total)
        y_ref[:, place, :] = pltpu.einshape("abc->bac", square)

    count = quarter // TILE

    def body(block, carry):
        cyclic, negative = product(0, block), product(1, block)
        for part, both in enumerate((cyclic + negative, cyclic - negative)):
            wide = product(2, block + part * count)
            left = part * quarter + block * TILE
            emit(left, both + wide)
            emit(left + DET, both - wide)
        return carry

    lax.fori_loop(0, count, body, 0, unroll=RAMP_UNROLL)


def ramp(x, high, low, done=(), total=0):
    blocks, rows, views, width = x.shape
    step = min(views, max(128 // rows, 8))
    if total:
        shape = (views, STITCH // 128 * total, 128)
        out_spec = pl.BlockSpec((step,) + shape[1:], lambda p: (p, 0, 0))
    else:
        shape = (rows, views, STITCH)
        out_spec = pl.BlockSpec((rows, step, STITCH), lambda p: (0, p, 0))
    band = pl.BlockSpec(high.shape, lambda p: (0, 0), pipeline_mode=pl.Buffered(1))
    return pl.pallas_call(
        functools.partial(ramp_kernel, total=total),
        out_shape=jax.ShapeDtypeStruct(shape, jnp.float32),
        grid=(views // step,),
        in_specs=[pl.BlockSpec((blocks, rows, step, width), lambda p: (0, 0, p, 0)), band, band]
        + [pl.BlockSpec((ref.shape[0], step, STITCH), lambda p: (0, p, 0)) for ref in done],
        out_specs=out_spec,
        compiler_params=pltpu.CompilerParams(vmem_limit_bytes=RAMP_VMEM),
        cost_estimate=pl.CostEstimate(
            flops=3 * 2 * rows * views * STITCH * 1536,
            bytes_accessed=8 * rows * views * STITCH + 4 * high.size,
            transcendentals=0,
        ),
        name="ramp",
    )(x, high, low, *done)


def shards(
    raw_counts,
    dark_frames,
    flat_frames,
    dark_index,
    flat_index,
    center_offset,
    blend_width,
    stripe_gain,
    ramp_window,
):
    devices = lax.axis_size("ang")
    half = devices // 2
    rows = raw_counts.shape[1]
    upper = lax.axis_index("ang") >= half
    offset = center_offset[0]
    spread = blend_width[0].astype(jnp.float32)

    as_lines = lambda frames: (
        frames.reshape(-1, rows, DET // 128, 128).transpose(0, 2, 1, 3).reshape(-1, rows * DET // 128, 128)
    )
    raw = as_lines(raw_counts).reshape(-1, 128)
    dark, flat = as_lines(dark_frames), as_lines(flat_frames)
    indices = (dark_index, flat_index)

    place = jnp.arange(DET, dtype=jnp.int32)
    first_low = jnp.where(upper, offset + 1, DET - offset)
    position = jnp.where(place >= first_low, place, place + DET).astype(jnp.float32)
    weight = jnp.clip((position - DET + 0.5 * spread) / spread, 0.0, 1.0)
    weight = jnp.where(upper, 1.0 - weight, weight)[None, :]
    scalars = jnp.stack([upper.astype(jnp.int32), first_low.astype(jnp.int32)])

    frequency = jnp.arange(DET + 1).astype(jnp.float32)
    stripe_line = ring_lines(impulse(stripe_gain, VIEWS))
    ramp_line = ring_lines(impulse(4.0 * frequency / STITCH * ramp_window, STITCH))
    stripe_high, stripe_low = bands(stripe_line, False)
    ramp_high, ramp_low = bands(ramp_line, True)

    groups = [list(range(half)), list(range(half, devices))]
    chunk = rows // CHUNKS
    done = []
    for start in range(0, rows, chunk):
        sent = prepare(scalars, indices, raw, dark, flat, weight, start, chunk, half)
        columns = lax.all_to_all(sent, "ang", 0, 0, axis_index_groups=groups, tiled=True)
        destriped = destripe(columns, stripe_high, stripe_low, devices)
        view_rows = lax.all_to_all(destriped, "ang", 0, 0, tiled=True)
        if start + chunk < rows:
            done.append(ramp(view_rows, ramp_high, ramp_low))
    lines = ramp(view_rows, ramp_high, ramp_low, done, rows)
    views = VIEWS // devices
    filtered = lines.reshape(views, STITCH // 128, rows, 128).transpose(0, 2, 1, 3)
    return filtered.reshape(views, rows, STITCH)


def solution(mesh):
    in_specs = (
        P("ang", "slab", None),
        P(None, "slab", None),
        P(None, "slab", None),
        P("ang"),
        P("ang"),
        P(),
        P(),
        P(),
        P(),
    )
    out_specs = P("ang", "slab", None)
    return jax.shard_map(shards, mesh=mesh, in_specs=in_specs, out_specs=out_specs, check_vma=False)
```

profile of v0, /device:TPU:15, one launch (start us, length us, event | category | flops | bytes accessed | tf_op | source)
XLA Modules:
  0.0 331.6 jit_solution(3224164714878332144)
XLA Ops:
  1.3 0.6 broadcast_select_fusion.weight_ref
  2.5 9.8 %prepare.3 = f32[8,2,256,256]{3,2,1,0:T(8,128)} custom-call(s32[2]{0:T(128)} %pad_add_fusion.scalars, s32[256]{0:T(256)} %dark_index.3, s32[256]{0:T(256)} %flat_index.3, f32[16384,128]{1,0:T(8,128)} %bitcast.47, f32[4,64,128]{2,1,0:T(8,128)} %bitcast.51, f32[8,64,128]{2,1,0:T(8,128)} %bitcast.49, f32[1,2048]{1,0:T(1,128)} %broadcast_select_fusion.weight_ref), custom_call_target="tpu_custom_call" | custom-call | flops 20971520 | bytes 12582912 | tf_op jit(solution)/shard_map/prepare/pallas_call | solution.py:174
  12.3 5.2 %all-to-all-start.2 = ((f32[8,2,256,256]{3,2,1,0:T(8,128)}), f32[8,2,256,256]{3,2,1,0:T(8,128)}, u32[]{:S(2)}, u32[]{:S(2)}) async-start(f32[8,2,256,256]{3,2,1,0:T(8,128)} %prepare.3), calls=%async_computation.2 | async-start | bytes 8388608 | tf_op jit(solution)/shard_map/all_to_all | solution.py:379
  17.5 9.8 %prepare.2 = f32[8,2,256,256]{3,2,1,0:T(8,128)} custom-call(s32[2]{0:T(128)} %pad_add_fusion.scalars, s32[256]{0:T(256)} %dark_index.3, s32[256]{0:T(256)} %flat_index.3, f32[16384,128]{1,0:T(8,128)} %bitcast.48, f32[4,64,128]{2,1,0:T(8,128)} %bitcast.52, f32[8,64,128]{2,1,0:T(8,128)} %bitcast.50, f32[1,2048]{1,0:T(1,128)} %broadcast_select_fusion.weight_ref), custom_call_target="tpu_custom_call" | custom-call | flops 20971520 | bytes 12582912 | tf_op jit(solution)/shard_map/prepare/pallas_call | solution.py:174
  27.4 36.4 %all-to-all-done.2.x_ref = f32[8,2,256,256]{3,2,1,0:T(8,128)} async-done(((f32[8,2,256,256]{3,2,1,0:T(8,128)}), f32[8,2,256,256]{3,2,1,0:T(8,128)}, u32[]{:S(2)}, u32[]{:S(2)}) %all-to-all-start.2) | async-done | bytes 4194336 | tf_op jit(solution)/shard_map/all_to_all | solution.py:379
  63.8 6.5 %all-to-all-start = ((f32[8,2,256,256]{3,2,1,0:T(8,128)}), f32[8,2,256,256]{3,2,1,0:T(8,128)}, u32[]{:S(2)}, u32[]{:S(2)}) async-start(f32[8,2,256,256]{3,2,1,0:T(8,128)} %prepare.2), calls=%async_computation | async-start | bytes 8388608 | tf_op jit(solution)/shard_map/all_to_all | solution.py:379
  70.9 0.6 broadcast_multiply_fusion.1
  73.0 0.6 bands.2
  73.6 8.4 %destripe.3 = f32[16,2,128,256]{3,2,1,0:T(8,128)} custom-call(f32[8,2,256,256]{3,2,1,0:T(8,128)} %all-to-all-done.2.x_ref, bf16[256,4096]{1,0:T(8,128)(2,1)S(1)} %get-tuple-element.9.high_ref, bf16[256,4096]{1,0:T(8,128)(2,1)S(1)} %get-tuple-element.10.low_ref), custom_call_target="tpu_custom_call" | custom-call | flops 4831838208 | bytes 12582912 | tf_op jit(solution)/shard_map/destripe/pallas_call | solution.py:239
  82.1 1.3 copy-done.2
  83.4 33.2 %all-to-all-done.x_ref = f32[8,2,256,256]{3,2,1,0:T(8,128)} async-done(((f32[8,2,256,256]{3,2,1,0:T(8,128)}), f32[8,2,256,256]{3,2,1,0:T(8,128)}, u32[]{:S(2)}, u32[]{:S(2)}) %all-to-all-start) | async-done | bytes 4194336 | tf_op jit(solution)/shard_map/all_to_all | solution.py:379
  116.5 6.8 %all-to-all-start.3 = ((f32[16,2,128,256]{3,2,1,0:T(8,128)}), f32[16,2,128,256]{3,2,1,0:T(8,128)}, u32[]{:S(2)}, u32[]{:S(2)}) async-start(f32[16,2,128,256]{3,2,1,0:T(8,128)} %destripe.3), calls=%async_computation.3 | async-start | bytes 8388608 | tf_op jit(solution)/shard_map/all_to_all | solution.py:381
  123.3 1.6 copy-done.3
  124.9 8.4 %destripe.2 = f32[16,2,128,256]{3,2,1,0:T(8,128)} custom-call(f32[8,2,256,256]{3,2,1,0:T(8,128)} %all-to-all-done.x_ref, bf16[256,4096]{1,0:T(8,128)(2,1)S(1)} %get-tuple-element.9.high_ref, bf16[256,4096]{1,0:T(8,128)(2,1)S(1)} %copy-done.3), custom_call_target="tpu_custom_call" | custom-call | flops 4831838208 | bytes 12582912 | tf_op jit(solution)/shard_map/destripe/pallas_call | solution.py:239
  133.4 82.4 %all-to-all-done.3.x_ref = f32[16,2,128,256]{3,2,1,0:T(8,128)} async-done(((f32[16,2,128,256]{3,2,1,0:T(8,128)}), f32[16,2,128,256]{3,2,1,0:T(8,128)}, u32[]{:S(2)}, u32[]{:S(2)}) %all-to-all-start.3) | async-done | bytes 4194336 | tf_op jit(solution)/shard_map/all_to_all | solution.py:381
  215.8 4.9 %all-to-all-start.1 = ((f32[16,2,128,256]{3,2,1,0:T(8,128)}), f32[16,2,128,256]{3,2,1,0:T(8,128)}, u32[]{:S(2)}, u32[]{:S(2)}) async-start(f32[16,2,128,256]{3,2,1,0:T(8,128)} %destripe.2), calls=%async_computation.1 | async-start | bytes 8388608 | tf_op jit(solution)/shard_map/all_to_all | solution.py:381
  221.4 0.6 broadcast_multiply_fusion
  223.1 2.3 bands.3
  225.4 2.0 copy-done
  227.4 1.9 copy-done.1
  229.3 14.9 %ramp.2.refs_0_ = f32[2,128,4096]{2,1,0:T(8,128)S(1)} custom-call(f32[16,2,128,256]{3,2,1,0:T(8,128)} %all-to-all-done.3.x_ref, bf16[8192,256]{1,0:T(8,128)(2,1)} %copy-done, bf16[8192,256]{1,0:T(8,128)(2,1)} %copy-done.1), custom_call_target="tpu_custom_call" | custom-call | flops 9663676416 | bytes 16777216 | tf_op jit(solution)/shard_map/ramp/pallas_call | solution.py:319
  244.2 2.0 copy-done.4
  246.2 67.0 %all-to-all-done.1.x_ref = f32[16,2,128,256]{3,2,1,0:T(8,128)} async-done(((f32[16,2,128,256]{3,2,1,0:T(8,128)}), f32[16,2,128,256]{3,2,1,0:T(8,128)}, u32[]{:S(2)}, u32[]{:S(2)}) %all-to-all-start.1) | async-done | bytes 4194336 | tf_op jit(solution)/shard_map/all_to_all | solution.py:381
  313.2 18.4 %ramp.3 = f32[128,128,128]{2,1,0:T(8,128)} custom-call(f32[16,2,128,256]{3,2,1,0:T(8,128)} %all-to-all-done.1.x_ref, bf16[8192,256]{1,0:T(8,128)(2,1)} %copy-done, bf16[8192,256]{1,0:T(8,128)(2,1)} %copy-done.1, f32[2,128,4096]{2,1,0:T(8,128)} %copy-done.4), custom_call_target="tpu_custom_call" | custom-call | flops 9663676416 | bytes 16777216 | tf_op jit(solution)/shard_map/ramp/pallas_call | solution.py:319
  (80 shorter events, 4.3 us)
Async XLA Ops:
  12.3 51.5 %all-to-all-start.2 = ((f32[8,2,256,256]{3,2,1,0:T(8,128)}), f32[8,2,256,256]{3,2,1,0:T(8,128)}, u32[]{:S(2)}, u32[]{:S(2)}) async-start(f32[8,2,256,256]{3,2,1,0:T(8,128)} %prepare.3), calls=%async_computation.2 | async-start | bytes 8388608 | tf_op jit(solution)/shard_map/all_to_all | solution.py:379
  27.3 43.0 %copy-start.18 = (f32[1025]{0:T(1024)S(1)}, f32[1025]{0:T(1024)}, u32[]{:S(2)}) copy-start(f32[1025]{0:T(1024)} %param.32) | copy-start | bytes 12304
  27.3 43.5 %copy-start.17 = (f32[1024]{0:T(1024)S(1)}, f32[1024]{0:T(1024)}, u32[]{:S(2)}) copy-start(f32[1024]{0:T(1024)} %constant.62.clone) | copy-start | bytes 12292
  27.3 43.6 %copy-start.20 = (f32[32]{0:T(128)S(1)}, f32[32]{0:T(128)}, u32[]{:S(2)}) copy-start(f32[32]{0:T(128)} %constant.69.clone) | copy-start | bytes 388
  27.3 44.2 %copy-start.14 = (f32[32,16]{1,0:T(8,128)S(1)}, f32[32,16]{1,0:T(8,128)}, u32[]{:S(2)}) copy-start(f32[32,16]{1,0:T(8,128)} %constant.64.clone) | copy-start | bytes 6148
  27.3 44.4 %copy-start.13 = (f32[32,16]{1,0:T(8,128)S(1)}, f32[32,16]{1,0:T(8,128)}, u32[]{:S(2)}) copy-start(f32[32,16]{1,0:T(8,128)} %constant.63.clone) | copy-start | bytes 6148
  27.3 44.5 %copy-start.5 = (f32[64,64]{1,0:T(8,128)S(1)}, f32[64,64]{1,0:T(8,128)}, u32[]{:S(2)}) copy-start(f32[64,64]{1,0:T(8,128)} %constant.67.clone) | copy-start | bytes 49156
  27.3 44.5 %copy-start.9 = (f32[32,64]{1,0:T(8,128)S(1)}, f32[32,64]{1,0:T(8,128)}, u32[]{:S(2)}) copy-start(f32[32,64]{1,0:T(8,128)} %constant.66.clone) | copy-start | bytes 24580
  27.4 44.5 %copy-start.10 = (f32[32,64]{1,0:T(8,128)S(1)}, f32[32,64]{1,0:T(8,128)}, u32[]{:S(2)}) copy-start(f32[32,64]{1,0:T(8,128)} %constant.65.clone) | copy-start | bytes 24580
  27.4 44.7 %copy-start.6 = (f32[64,64]{1,0:T(8,128)S(1)}, f32[64,64]{1,0:T(8,128)}, u32[]{:S(2)}) copy-start(f32[64,64]{1,0:T(8,128)} %constant.68.clone) | copy-start | bytes 49156
  63.8 52.7 %all-to-all-start = ((f32[8,2,256,256]{3,2,1,0:T(8,128)}), f32[8,2,256,256]{3,2,1,0:T(8,128)}, u32[]{:S(2)}, u32[]{:S(2)}) async-start(f32[8,2,256,256]{3,2,1,0:T(8,128)} %prepare.2), calls=%async_computation | async-start | bytes 8388608 | tf_op jit(solution)/shard_map/all_to_all | solution.py:379
  116.5 99.2 %all-to-all-start.3 = ((f32[16,2,128,256]{3,2,1,0:T(8,128)}), f32[16,2,128,256]{3,2,1,0:T(8,128)}, u32[]{:S(2)}, u32[]{:S(2)}) async-start(f32[16,2,128,256]{3,2,1,0:T(8,128)} %destripe.3), calls=%async_computation.3 | async-start | bytes 8388608 | tf_op jit(solution)/shard_map/all_to_all | solution.py:381
  123.3 1.6 copy-start.3
  133.3 87.4 %copy-start.15 = (f32[2049]{0:T(1024)S(1)}, f32[2049]{0:T(1024)}, u32[]{:S(2)}) copy-start(f32[2049]{0:T(1024)} %param.33) | copy-start | bytes 24592
  133.3 88.0 %copy-start.16 = (f32[2048]{0:T(1024)S(1)}, f32[2048]{0:T(1024)}, u32[]{:S(2)}) copy-start(f32[2048]{0:T(1024)} %constant.70.clone) | copy-start | bytes 24580
  133.3 88.1 %copy-start.19 = (f32[64]{0:T(128)S(1)}, f32[64]{0:T(128)}, u32[]{:S(2)}) copy-start(f32[64]{0:T(128)} %constant.75.clone) | copy-start | bytes 772
  133.3 88.7 %copy-start.12 = (f32[64,32]{1,0:T(8,128)S(1)}, f32[64,32]{1,0:T(8,128)}, u32[]{:S(2)}) copy-start(f32[64,32]{1,0:T(8,128)} %constant.72.clone) | copy-start | bytes 24580
  133.3 88.9 %copy-start.11 = (f32[64,32]{1,0:T(8,128)S(1)}, f32[64,32]{1,0:T(8,128)}, u32[]{:S(2)}) copy-start(f32[64,32]{1,0:T(8,128)} %constant.71.clone) | copy-start | bytes 24580
  133.3 89.0 %copy-start.7 = (f32[64,64]{1,0:T(8,128)S(1)}, f32[64,64]{1,0:T(8,128)}, u32[]{:S(2)}) copy-start(f32[64,64]{1,0:T(8,128)} %constant.74.clone) | copy-start | bytes 49156
  133.3 89.0 %copy-start.8 = (f32[64,64]{1,0:T(8,128)S(1)}, f32[64,64]{1,0:T(8,128)}, u32[]{:S(2)}) copy-start(f32[64,64]{1,0:T(8,128)} %constant.73.clone) | copy-start | bytes 49156
  215.8 97.4 %all-to-all-start.1 = ((f32[16,2,128,256]{3,2,1,0:T(8,128)}), f32[16,2,128,256]{3,2,1,0:T(8,128)}, u32[]{:S(2)}, u32[]{:S(2)}) async-start(f32[16,2,128,256]{3,2,1,0:T(8,128)} %destripe.2), calls=%async_computation.1 | async-start | bytes 8388608 | tf_op jit(solution)/shard_map/all_to_all | solution.py:381
  225.3 2.0 copy-start
  227.4 1.9 copy-start.1
  244.2 2.0 copy-start.4
  (1 other events, 1.3 us)
where the time goes:
time: 332 us
  waiting for transfers between devices  219 us (66%)
  Pallas kernels  72.6 us (22%)
  starting transfers between devices  23.3 us (7%)
  local copies, waits for them, and re-layouts  11.1 us (3%)
    all_to_all x2, waiting for transfers between devices, shards(): view_rows = lax.all_to_all(destriped, 'ang', 0, 0, tiled=True)  149 us
    all_to_all x2, waiting for transfers between devices, shards(): lax.all_to_all(sent, 'ang', 0, 0, axis_index_groups=groups, tiled=True)  69.6 us
    pallas_call x2, Pallas kernels, ramp(): pl.pallas_call(functools.partial(ramp_kernel, total=total), out_shape=jax...  33.4 us
    pallas_call x2, Pallas kernels, prepare(): pl.pallas_call(functools.partial(prepare_kernel, start=start), out_shape=...  19.6 us
    pallas_call x2, Pallas kernels, destripe(): pl.pallas_call(destripe_kernel, out_shape=jax.ShapeDtypeStruct((devices,...  16.8 us
    all_to_all x2, starting transfers between devices, shards(): view_rows = lax.all_to_all(destriped, 'ang', 0, 0, tiled=True)  11.7 us
    all_to_all x2, starting transfers between devices, shards(): lax.all_to_all(sent, 'ang', 0, 0, axis_index_groups=groups, tiled=True)  11.6 us
    unnamed x48, local copies, waits for them, and re-layouts  8.93 us
  transfers between devices with their start and end apart: 4, of which 4 were waited for; matrix products, arithmetic and copies ran while one was open for 1% of the time, Pallas kernels for 13%

commit v1 on v0

--- a/solution.py
+++ b/solution.py
@@ -13,14 +13,17 @@
 STITCH = 2 * DET
 EDGE = 64
 TILE = 256
-CHUNKS = 2
+CHUNKS = [2, 2]
+HELD = 5
+KEPT = 3
+CROSS = True
 STEP = 128
 UNROLL = 4
 STRIPE_UNROLL = 2
 RAMP_UNROLL = 4
 MIB = 1024 * 1024
-RAMP_VMEM = 48 * MIB
-STRIPE_VMEM = 48 * MIB
+RAMP_VMEM = 36 * MIB
+STRIPE_VMEM = 40 * MIB
 PREPARE_VMEM = 56 * MIB
 
 precise = lax.Precision.HIGHEST
@@ -200,7 +203,8 @@
     return pl.ds(pl.multiple_of(start + size - TILE - TILE * block, TILE), size)
 
 
-def destripe_kernel(x_ref, high_ref, low_ref, y_ref, full_ref):
+def destripe_kernel(scalars, x_ref, high_ref, low_ref, *refs):
+    *out_refs, full_ref = refs
     width = x_ref.shape[3]
     quarter = VIEWS // 4
     x = x_ref[...].reshape(4, quarter, width)
@@ -229,20 +233,38 @@
         return carry
 
     lax.fori_loop(0, count, body, 0, unroll=STRIPE_UNROLL)
-    y_ref[...] = full_ref[...].reshape(y_ref.shape)
-
-
-def destripe(x, high, low, devices):
+    if len(out_refs) == 1:
+        out_refs[0][...] = full_ref[...].reshape(out_refs[0].shape)
+        return
+    half = len(out_refs) // 2
+    views = out_refs[0].shape[1]
+    upper, me = scalars[0], scalars[1]
+    for place, out_ref in enumerate(out_refs):
+        side = upper if place < half else 1 - upper
+        owner = side * half + (me ^ place % half)
+        out_ref[0] = full_ref[pl.ds(pl.multiple_of(owner * views, views), views), :]
+
+
+def destripe(scalars, x, high, low, devices, crossing):
     count, rows, share, width = x.shape
     views = VIEWS // devices
-    band = pl.BlockSpec(high.shape, lambda r: (0, 0), pipeline_mode=pl.Buffered(1))
+    if crossing:
+        shapes = [jax.ShapeDtypeStruct((rows, views, width), jnp.float32)] * devices
+        out_specs = [pl.BlockSpec((1, views, width), lambda r, s: (r, 0, 0))] * devices
+    else:
+        shapes = [jax.ShapeDtypeStruct((devices, rows, views, width), jnp.float32)]
+        out_specs = [pl.BlockSpec((devices, 1, views, width), lambda r, s: (0, r, 0, 0))]
+    band = pl.BlockSpec(high.shape, lambda r, s: (0, 0), pipeline_mode=pl.Buffered(1))
     return pl.pallas_call(
         destripe_kernel,
-        out_shape=jax.ShapeDtypeStruct((devices, rows, views, width), jnp.float32),
-        grid=(rows,),
-        in_specs=[pl.BlockSpec((count, 1, share, width), lambda r: (0, r, 0, 0)), band, band],
-        out_specs=pl.BlockSpec((devices, 1, views, width), lambda r: (0, r, 0, 0)),
-        scratch_shapes=[pltpu.VMEM((VIEWS, width), jnp.float32)],
+        out_shape=shapes,
+        grid_spec=pltpu.PrefetchScalarGridSpec(
+            num_scalar_prefetch=1,
+            grid=(rows,),
+            in_specs=[pl.BlockSpec((count, 1, share, width), lambda r, s: (0, r, 0, 0)), band, band],
+            out_specs=out_specs,
+            scratch_shapes=[pltpu.VMEM((VIEWS, width), jnp.float32)],
+        ),
         compiler_params=pltpu.CompilerParams(vmem_limit_bytes=STRIPE_VMEM),
         cost_estimate=pl.CostEstimate(
             flops=3 * 2 * rows * width * VIEWS * 768,
@@ -250,22 +272,32 @@
             transcendentals=0,
         ),
         name="destripe",
-    )(x, high, low)
-
-
-def ramp_kernel(x_ref, high_ref, low_ref, *refs, total):
-    *done_refs, y_ref = refs
-    blocks, rows, views, width = x_ref.shape
-    half = blocks // 2
+    )(scalars, x, high, low)
+
+
+def ramp_kernel(scalars, *refs, total, parts):
+    part_refs, refs = refs[:parts], refs[parts:]
+    high_ref, low_ref, *done_refs, y_ref, full_ref = refs
+    rows, views, width = part_refs[0].shape[-3:]
     depth = rows * views
-    pieces = [x_ref[block].reshape(depth, width) for block in range(blocks)]
-    direct = jnp.concatenate(pieces[:half], axis=1)
-    partner = jnp.concatenate(pieces[half:], axis=1)
+    upper, me = scalars[0], scalars[1]
+    half = DET // width
+    if parts > 1:
+        for turn, part_ref in enumerate(part_refs):
+            place = pl.ds(pl.multiple_of((me ^ turn % half) * width, 128), width)
+            full_ref[turn // half, :, place] = part_ref[...].reshape(depth, width)
+        own, other = full_ref[0], full_ref[1]
+    else:
+        pieces = [part_refs[0][block].reshape(depth, width) for block in range(2 * half)]
+        own = jnp.concatenate(pieces[:half], axis=1)
+        other = jnp.concatenate(pieces[half:], axis=1)
     place = lax.broadcasted_iota(jnp.int32, (1, DET), 1)
     direct_sign = jnp.where(place >= DET - EDGE, 1.0, -1.0)
     partner_sign = jnp.where(place < EDGE, -1.0, 1.0)
-    added = direct + partner
-    wide = direct * direct_sign + partner * partner_sign
+    own_sign = jnp.where(upper != 0, partner_sign, direct_sign)
+    other_sign = jnp.where(upper != 0, direct_sign, partner_sign)
+    added = own + other
+    wide = own * own_sign + other * other_sign
     quarter = DET // 2
     left_half, right_half = added[:, :quarter], added[:, quarter:]
     rings = [split(ring) for ring in (left_half + right_half, left_half - right_half, wide)]
@@ -306,23 +338,29 @@
     lax.fori_loop(0, count, body, 0, unroll=RAMP_UNROLL)
 
 
-def ramp(x, high, low, done=(), total=0):
-    blocks, rows, views, width = x.shape
-    step = min(views, max(128 // rows, 8))
+def ramp(scalars, parts, high, low, done=(), total=0):
+    rows, views, width = parts[0].shape[-3:]
+    step = min(views, max(128 // pl.next_power_of_2(rows), 8))
     if total:
         shape = (views, STITCH // 128 * total, 128)
-        out_spec = pl.BlockSpec((step,) + shape[1:], lambda p: (p, 0, 0))
+        out_spec = pl.BlockSpec((step,) + shape[1:], lambda p, s: (p, 0, 0))
     else:
         shape = (rows, views, STITCH)
-        out_spec = pl.BlockSpec((rows, step, STITCH), lambda p: (0, p, 0))
-    band = pl.BlockSpec(high.shape, lambda p: (0, 0), pipeline_mode=pl.Buffered(1))
+        out_spec = pl.BlockSpec((rows, step, STITCH), lambda p, s: (0, p, 0))
+    band = pl.BlockSpec(high.shape, lambda p, s: (0, 0), pipeline_mode=pl.Buffered(1))
+    middle = lambda ref: pl.BlockSpec(
+        ref.shape[:-2] + (step, ref.shape[-1]), lambda p, s: (0,) * (ref.ndim - 2) + (p, 0)
+    )
     return pl.pallas_call(
-        functools.partial(ramp_kernel, total=total),
+        functools.partial(ramp_kernel, total=total, parts=len(parts)),
         out_shape=jax.ShapeDtypeStruct(shape, jnp.float32),
-        grid=(views // step,),
-        in_specs=[pl.BlockSpec((blocks, rows, step, width), lambda p: (0, 0, p, 0)), band, band]
-        + [pl.BlockSpec((ref.shape[0], step, STITCH), lambda p: (0, p, 0)) for ref in done],
-        out_specs=out_spec,
+        grid_spec=pltpu.PrefetchScalarGridSpec(
+            num_scalar_prefetch=1,
+            grid=(views // step,),
+            in_specs=[middle(ref) for ref in parts] + [band, band] + [middle(ref) for ref in done],
+            out_specs=out_spec,
+            scratch_shapes=[pltpu.VMEM((2, rows * step, DET), jnp.float32)],
+        ),
         compiler_params=pltpu.CompilerParams(vmem_limit_bytes=RAMP_VMEM),
         cost_estimate=pl.CostEstimate(
             flops=3 * 2 * rows * views * STITCH * 1536,
@@ -330,7 +368,7 @@
             transcendentals=0,
         ),
         name="ramp",
-    )(x, high, low, *done)
+    )(scalars, *parts, high, low, *done)
 
 
 def shards(
@@ -372,16 +410,44 @@
     ramp_high, ramp_low = bands(ramp_line, True)
 
     groups = [list(range(half)), list(range(half, devices))]
-    chunk = rows // CHUNKS
+    crossing = CROSS and DET // half >= 128
+    sides = jnp.stack([upper.astype(jnp.int32), lax.axis_index("ang") % half])
+    sides = sides if crossing else jnp.zeros_like(sides)
+
+    def deliver(part, place):
+        flip, turn = place // half, place % half
+        if place == 0:
+            return part
+        pairs = [(src, (src // half ^ flip) * half + (src % half ^ turn)) for src in range(devices)]
+        return lax.ppermute(part, "ang", pairs)
+
+    sizes = CHUNKS if sum(CHUNKS) == rows else [rows]
+    starts = [sum(sizes[:i]) for i in range(len(sizes))]
+    fresh, crossed, parts = [], [], []
+    for i, (start, size) in enumerate(zip(starts, sizes)):
+        sent = prepare(scalars, indices, raw, dark, flat, weight, start, size, half)
+        if i == 1:
+            sent, stripe_high, stripe_low = lax.optimization_barrier((sent, stripe_high, stripe_low))
+        columns = lax.all_to_all(sent, "ang", 0, 0, axis_index_groups=groups, tiled=True)
+        if crossing and i >= 1:
+            columns, crossed[i - 1][:HELD] = lax.optimization_barrier((columns, crossed[i - 1][:HELD]))
+        fresh.append(destripe(sides, columns, stripe_high, stripe_low, devices, crossing))
+        if crossing:
+            crossed.append([deliver(part, half + place) for place, part in enumerate(fresh[i][half:])])
+    for i, pieces in enumerate(fresh):
+        if not crossing:
+            parts.append([lax.all_to_all(pieces[0], "ang", 0, 0, tiled=True)])
+            continue
+        own = pieces[:half]
+        if i + 1 < len(sizes) and KEPT > 0:
+            own, crossed[i + 1][:KEPT] = lax.optimization_barrier((own, crossed[i + 1][:KEPT]))
+        elif i + 1 < len(sizes):
+            own, _ = lax.optimization_barrier((own, fresh[i + 1][0]))
+        parts.append([deliver(part, place) for place, part in enumerate(own)] + crossed[i])
     done = []
-    for start in range(0, rows, chunk):
-        sent = prepare(scalars, indices, raw, dark, flat, weight, start, chunk, half)
-        columns = lax.all_to_all(sent, "ang", 0, 0, axis_index_groups=groups, tiled=True)
-        destriped = destripe(columns, stripe_high, stripe_low, devices)
-        view_rows = lax.all_to_all(destriped, "ang", 0, 0, tiled=True)
-        if start + chunk < rows:
-            done.append(ramp(view_rows, ramp_high, ramp_low))
-    lines = ramp(view_rows, ramp_high, ramp_low, done, rows)
+    for pieces in parts[:-1]:
+        done.append(ramp(sides, pieces, ramp_high, ramp_low))
+    lines = ramp(sides, parts[-1], ramp_high, ramp_low, done, rows)
     views = VIEWS // devices
     filtered = lines.reshape(views, STITCH // 128, rows, 128).transpose(0, 2, 1, 3)
     return filtered.reshape(views, rows, STITCH)

time: 332 us -> 327 us (0.985)
  waiting for transfers between devices: 219 us -> 153 us
  starting transfers between devices: 23.3 us -> 76.4 us
  local copies, waits for them, and re-layouts: 11.1 us -> 19 us
    all_to_all x2 -> x0, waiting for transfers between devices: 149 us -> none  [shards(): view_rows = lax.all_to_all(destriped, 'ang', 0, 0, tiled=True)]
    ppermute x0 -> x30, waiting for transfers between devices: none -> 114 us  [deliver(): return lax.ppermute(part, 'ang', pairs)]
    ppermute x0 -> x30, starting transfers between devices: none -> 64.5 us  [deliver(): return lax.ppermute(part, 'ang', pairs)]
    all_to_all x2, waiting for transfers between devices: 69.6 us -> 39.2 us  [shards(): lax.all_to_all(sent, 'ang', 0, 0, axis_index_groups=groups, tiled=True)]
    all_to_all x2 -> x0, starting transfers between devices: 11.7 us -> none  [shards(): view_rows = lax.all_to_all(destriped, 'ang', 0, 0, tiled=True)]
    unnamed x48 -> x82, local copies, waits for them, and re-layouts: 8.93 us -> 16.8 us
  transfers between devices with their start and end apart: 4 -> 32, of which waited for: 4 -> 17; matrix products, arithmetic and copies ran while one was open for 1% -> 2% of each run, Pallas kernels for 13% -> 13%
where the time goes in v1:
time: 327 us; the launch traced here: 324 us
  waiting for transfers between devices  153 us (47%)
  starting transfers between devices  76.4 us (23%)
  Pallas kernels  69.4 us (21%)
  local copies, waits for them, and re-layouts  19 us (6%)
    ppermute x30, waiting for transfers between devices, deliver(): return lax.ppermute(part, 'ang', pairs)  114 us
    ppermute x30, starting transfers between devices, deliver(): return lax.ppermute(part, 'ang', pairs)  64.5 us
    all_to_all x2, waiting for transfers between devices, shards(): lax.all_to_all(sent, 'ang', 0, 0, axis_index_groups=groups, tiled=True)  39.2 us
    pallas_call x2, Pallas kernels, ramp(): pl.pallas_call(functools.partial(ramp_kernel, total=total, parts=len(part...  29.5 us
    pallas_call x2, Pallas kernels, prepare(): pl.pallas_call(functools.partial(prepare_kernel, start=start), out_shape=...  19.6 us
    pallas_call x2, Pallas kernels, destripe(): pl.pallas_call(destripe_kernel, out_shape=shapes, grid_spec=pltpu.Prefetc...  17.4 us
    unnamed x82, local copies, waits for them, and re-layouts  16.8 us
    all_to_all x2, starting transfers between devices, shards(): lax.all_to_all(sent, 'ang', 0, 0, axis_index_groups=groups, tiled=True)  11.8 us
  transfers between devices with their start and end apart: 32, of which 17 were waited for; matrix products, arithmetic and copies ran while one was open for 2% of the time, Pallas kernels for 13%

profile of v1, /device:TPU:15, one launch (start us, length us, event | category | flops | bytes accessed | tf_op | source)
XLA Modules:
  0.0 323.9 jit_solution(10466899627869594095)
XLA Ops:
  2.6 9.8 %prepare.3 = f32[8,2,256,256]{3,2,1,0:T(8,128)} custom-call(s32[2]{0:T(128)} %pad_add_fusion.1.scalars, s32[256]{0:T(256)} %dark_index.3, s32[256]{0:T(256)} %flat_index.3, f32[16384,128]{1,0:T(8,128)} %bitcast.48, f32[4,64,128]{2,1,0:T(8,128)} %bitcast.52, f32[8,64,128]{2,1,0:T(8,128)} %bitcast.50, f32[1,2048]{1,0:T(1,128)} %broadcast_select_fusion.weight_ref), custom_call_target="tpu_custom_call" | custom-call | flops 20971520 | bytes 12582912 | tf_op jit(solution)/shard_map/prepare/pallas_call | solution.py:177
  12.5 5.4 %all-to-all-start.1 = ((f32[8,2,256,256]{3,2,1,0:T(8,128)}), f32[8,2,256,256]{3,2,1,0:T(8,128)}, u32[]{:S(2)}, u32[]{:S(2)}) async-start(f32[8,2,256,256]{3,2,1,0:T(8,128)} %prepare.3), calls=%async_computation.1 | async-start | bytes 8388608 | tf_op jit(solution)/shard_map/all_to_all | solution.py:431
  22.5 9.8 %prepare.2 = f32[8,2,256,256]{3,2,1,0:T(8,128)} custom-call(s32[2]{0:T(128)} %pad_add_fusion.1.scalars, s32[256]{0:T(256)} %dark_index.3, s32[256]{0:T(256)} %flat_index.3, f32[16384,128]{1,0:T(8,128)} %bitcast.49, f32[4,64,128]{2,1,0:T(8,128)} %bitcast.53, f32[8,64,128]{2,1,0:T(8,128)} %bitcast.51, f32[1,2048]{1,0:T(1,128)} %broadcast_select_fusion.weight_ref), custom_call_target="tpu_custom_call" | custom-call | flops 20971520 | bytes 12582912 | tf_op jit(solution)/shard_map/prepare/pallas_call | solution.py:177
  32.3 31.9 %all-to-all-done.1.x_ref = f32[8,2,256,256]{3,2,1,0:T(8,128)} async-done(((f32[8,2,256,256]{3,2,1,0:T(8,128)}), f32[8,2,256,256]{3,2,1,0:T(8,128)}, u32[]{:S(2)}, u32[]{:S(2)}) %all-to-all-start.1) | async-done | bytes 4194336 | tf_op jit(solution)/shard_map/all_to_all | solution.py:431
  64.1 6.5 %all-to-all-start = ((f32[8,2,256,256]{3,2,1,0:T(8,128)}), f32[8,2,256,256]{3,2,1,0:T(8,128)}, u32[]{:S(2)}, u32[]{:S(2)}) async-start(f32[8,2,256,256]{3,2,1,0:T(8,128)} %prepare.2), calls=%async_computation | async-start | bytes 8388608 | tf_op jit(solution)/shard_map/all_to_all | solution.py:431
  72.4 8.8 %destripe.2 = (f32[2,128,256]{2,1,0:T(8,128)S(1)}, f32[2,128,256]{2,1,0:T(8,128)S(1)}, f32[2,128,256]{2,1,0:T(8,128)S(1)}, f32[2,128,256]{2,1,0:T(8,128)S(1)}, f...) custom-call(s32[2]{0:T(128)S(1)} %pad_add_fusion.scalars, ...), custom_call_target="tpu_custom_call" | custom-call | flops 4831838208 | bytes 12582912 | tf_op jit(solution)/shard_map/destripe/pallas_call | solution.py:258
  94.6 29.8 %collective-permute-done.refs_8_ = f32[2,128,256]{2,1,0:T(8,128)S(1)} collective-permute-done((f32[2,128,256]{2,1,0:T(8,128)S(1)}, f32[2,128,256]{2,1,0:T(8,128)S(1)}, u32[]{:S(2)}, u32[]{:S(2)}) %collective-permute-start) | collective-permute-done | bytes 262176 | tf_op jit(solution)/shard_map/ppermute | solution.py:422
  124.9 6.1 %collective-permute-done.1.refs_9_ = f32[2,128,256]{2,1,0:T(8,128)S(1)} collective-permute-done((f32[2,128,256]{2,1,0:T(8,128)S(1)}, f32[2,128,256]{2,1,0:T(8,128)S(1)}, u32[]{:S(2)}, u32[]{:S(2)}) %collective-permute-start.1) | collective-permute-done | bytes 262176 | tf_op jit(solution)/shard_map/ppermute | solution.py:422
  131.0 7.3 %all-to-all-done.x_ref = f32[8,2,256,256]{3,2,1,0:T(8,128)} async-done(((f32[8,2,256,256]{3,2,1,0:T(8,128)}), f32[8,2,256,256]{3,2,1,0:T(8,128)}, u32[]{:S(2)}, u32[]{:S(2)}) %all-to-all-start) | async-done | bytes 4194336 | tf_op jit(solution)/shard_map/all_to_all | solution.py:431
  143.6 8.7 %destripe.3 = (f32[2,128,256]{2,1,0:T(8,128)S(1)}, f32[2,128,256]{2,1,0:T(8,128)}, f32[2,128,256]{2,1,0:T(8,128)}, f32[2,128,256]{2,1,0:T(8,128)}, f32[2,128,256...) custom-call(s32[2]{0:T(128)S(1)} %pad_add_fusion.scalars, ...), custom_call_target="tpu_custom_call" | custom-call | flops 4831838208 | bytes 12582912 | tf_op jit(solution)/shard_map/destripe/pallas_call | solution.py:258
  158.6 5.1 %collective-permute-start.12 = (f32[2,128,256]{2,1,0:T(8,128)S(1)}, f32[2,128,256]{2,1,0:T(8,128)S(1)}, u32[]{:S(2)}, u32[]{:S(2)}) collective-permute-start(f32[2,128,256]{2,1,0:T(8,128)S(1)} %get-tuple-element.88), channel_id=1, source_target_pairs={{0,8},{1,9},{2,10},{3,11},{4,12},{5,13},{6,14},{7,15},{8,0},{9,1},... | collective-permute-start | bytes 786440 | tf_op jit(solution)/shard_map/ppermute | solution.py:422
  163.7 13.0 %collective-permute-start.13 = (f32[2,128,256]{2,1,0:T(8,128)S(1)}, f32[2,128,256]{2,1,0:T(8,128)S(1)}, u32[]{:S(2)}, u32[]{:S(2)}) collective-permute-start(f32[2,128,256]{2,1,0:T(8,128)S(1)} %get-tuple-element.89), channel_id=1, source_target_pairs={{0,9},{1,8},{2,11},{3,10},{4,13},{5,12},{6,15},{7,14},{8,1},{9,0},... | collective-permute-start | bytes 786440 | tf_op jit(solution)/shard_map/ppermute | solution.py:422
  181.6 21.0 %collective-permute-done.13.refs_9_ = f32[2,128,256]{2,1,0:T(8,128)S(1)} collective-permute-done((f32[2,128,256]{2,1,0:T(8,128)S(1)}, f32[2,128,256]{2,1,0:T(8,128)S(1)}, u32[]{:S(2)}, u32[]{:S(2)}) %collective-permute-start.13) | collective-permute-done | bytes 262176 | tf_op jit(solution)/shard_map/ppermute | solution.py:422
  202.5 7.6 %collective-permute-start.7 = (f32[2,128,256]{2,1,0:T(8,128)}, f32[2,128,256]{2,1,0:T(8,128)S(1)}, u32[]{:S(2)}, u32[]{:S(2)}) collective-permute-start(f32[2,128,256]{2,1,0:T(8,128)} %get-tuple-element.75), channel_id=1, source_target_pairs={{0,3},{1,2},{2,1},{3,0},{4,7},{5,6},{6,5},{7,4},{8,11},{9,10},{10,... | collective-permute-start | bytes 786440 | tf_op jit(solution)/shard_map/ppermute | solution.py:422
  211.5 6.2 %collective-permute-done.29.refs_15_ = f32[2,128,256]{2,1,0:T(8,128)S(1)} collective-permute-done((f32[2,128,256]{2,1,0:T(8,128)}, f32[2,128,256]{2,1,0:T(8,128)S(1)}, u32[]{:S(2)}, u32[]{:S(2)}) %collective-permute-start.29) | collective-permute-done | bytes 262176 | tf_op jit(solution)/shard_map/ppermute | solution.py:422
  228.1 4.8 %collective-permute-done.10.refs_6_ = f32[2,128,256]{2,1,0:T(8,128)} collective-permute-done((f32[2,128,256]{2,1,0:T(8,128)}, f32[2,128,256]{2,1,0:T(8,128)}, u32[]{:S(2)}, u32[]{:S(2)}) %collective-permute-start.10) | collective-permute-done | bytes 262176 | tf_op jit(solution)/shard_map/ppermute | solution.py:422
  232.8 6.0 %collective-permute-done.11.refs_7_ = f32[2,128,256]{2,1,0:T(8,128)} collective-permute-done((f32[2,128,256]{2,1,0:T(8,128)}, f32[2,128,256]{2,1,0:T(8,128)}, u32[]{:S(2)}, u32[]{:S(2)}) %collective-permute-start.11) | collective-permute-done | bytes 262176 | tf_op jit(solution)/shard_map/ppermute | solution.py:422
  249.9 9.5 %collective-permute-start.17 = (f32[2,128,256]{2,1,0:T(8,128)}, f32[2,128,256]{2,1,0:T(8,128)S(1)}, u32[]{:S(2)}, u32[]{:S(2)}) collective-permute-start(f32[2,128,256]{2,1,0:T(8,128)} %copy-done.9), channel_id=1, source_target_pairs={{0,13},{1,12},{2,15},{3,14},{4,9},{5,8},{6,11},{7,10},{8,5},{9,4},... | collective-permute-start | bytes 786440 | tf_op jit(solution)/shard_map/ppermute | solution.py:422
  268.1 13.4 %ramp.2.refs_18_ = f32[2,128,4096]{2,1,0:T(8,128)S(1)} custom-call(s32[2]{0:T(128)S(1)} %pad_add_fusion.scalars, f32[2,128,256]{2,1,0:T(8,128)S(1)} %copy-done.18, f32[2,128,256]{2,1,0:T(8,128)} %collective-permute-done.20.refs_1_, f32[2,128,256]{2,1,0:T(8,128)} %collective-permute-done.21.refs_2_, f32[2,128,256]{2,1,0:T(8,128)} %collective-permute-done.22.refs_3_, ...), custom_call_target="tpu_custom_call" | custom-call | flops 9663676416 | bytes 16777216 | tf_op jit(solution)/shard_map/ramp/pallas_call | solution.py:354
  281.6 4.9 %collective-permute-done.16.refs_12_ = f32[2,128,256]{2,1,0:T(8,128)S(1)} collective-permute-done((f32[2,128,256]{2,1,0:T(8,128)}, f32[2,128,256]{2,1,0:T(8,128)S(1)}, u32[]{:S(2)}, u32[]{:S(2)}) %collective-permute-start.16) | collective-permute-done | bytes 262176 | tf_op jit(solution)/shard_map/ppermute | solution.py:422
  286.5 9.6 %collective-permute-done.17.refs_13_ = f32[2,128,256]{2,1,0:T(8,128)S(1)} collective-permute-done((f32[2,128,256]{2,1,0:T(8,128)}, f32[2,128,256]{2,1,0:T(8,128)S(1)}, u32[]{:S(2)}, u32[]{:S(2)}) %collective-permute-start.17) | collective-permute-done | bytes 262176 | tf_op jit(solution)/shard_map/ppermute | solution.py:422
  296.1 6.1 %collective-permute-done.18.refs_14_ = f32[2,128,256]{2,1,0:T(8,128)S(1)} collective-permute-done((f32[2,128,256]{2,1,0:T(8,128)}, f32[2,128,256]{2,1,0:T(8,128)S(1)}, u32[]{:S(2)}, u32[]{:S(2)}) %collective-permute-start.18) | collective-permute-done | bytes 262176 | tf_op jit(solution)/shard_map/ppermute | solution.py:422
  302.3 5.6 %collective-permute-done.19.refs_15_ = f32[2,128,256]{2,1,0:T(8,128)S(1)} collective-permute-done((f32[2,128,256]{2,1,0:T(8,128)}, f32[2,128,256]{2,1,0:T(8,128)S(1)}, u32[]{:S(2)}, u32[]{:S(2)}) %collective-permute-start.19) | collective-permute-done | bytes 262176 | tf_op jit(solution)/shard_map/ppermute | solution.py:422
  307.9 16.0 %ramp.3 = f32[128,128,128]{2,1,0:T(8,128)} custom-call(s32[2]{0:T(128)S(1)} %pad_add_fusion.scalars, f32[2,128,256]{2,1,0:T(8,128)S(1)} %copy-done.20, f32[2,128,256]{2,1,0:T(8,128)S(1)} %collective-permute-done.5.refs_1_, f32[2,128,256]{2,1,0:T(8,128)S(1)} %collective-permute-done.6.refs_2_, f32[2,128,256]{2,1,0:T(8,128)S(1)} %collective-permute-done.7.refs_3_, ...), custom_call_target="tpu_custom_call" | custom-call | flops 9663676416 | bytes 16777216 | tf_op jit(solution)/shard_map/ramp/pallas_call | solution.py:354
  (171 shorter events, 69.4 us)
Async XLA Ops:
  12.5 51.6 %all-to-all-start.1 = ((f32[8,2,256,256]{3,2,1,0:T(8,128)}), f32[8,2,256,256]{3,2,1,0:T(8,128)}, u32[]{:S(2)}, u32[]{:S(2)}) async-start(f32[8,2,256,256]{3,2,1,0:T(8,128)} %prepare.3), calls=%async_computation.1 | async-start | bytes 8388608 | tf_op jit(solution)/shard_map/all_to_all | solution.py:431
  64.1 74.3 %all-to-all-start = ((f32[8,2,256,256]{3,2,1,0:T(8,128)}), f32[8,2,256,256]{3,2,1,0:T(8,128)}, u32[]{:S(2)}, u32[]{:S(2)}) async-start(f32[8,2,256,256]{3,2,1,0:T(8,128)} %prepare.2), calls=%async_computation | async-start | bytes 8388608 | tf_op jit(solution)/shard_map/all_to_all | solution.py:431
  86.1 38.3 %collective-permute-start = (f32[2,128,256]{2,1,0:T(8,128)S(1)}, f32[2,128,256]{2,1,0:T(8,128)S(1)}, u32[]{:S(2)}, u32[]{:S(2)}) collective-permute-start(f32[2,128,256]{2,1,0:T(8,128)S(1)} %get-tuple-element.64), channel_id=1, source_target_pairs={{0,8},{1,9},{2,10},{3,11},{4,12},{5,13},{6,14},{7,15},{8,0},{9,1},... | collective-permute-start | bytes 786440 | tf_op jit(solution)/shard_map/ppermute | solution.py:422
  88.4 42.6 %collective-permute-start.1 = (f32[2,128,256]{2,1,0:T(8,128)S(1)}, f32[2,128,256]{2,1,0:T(8,128)S(1)}, u32[]{:S(2)}, u32[]{:S(2)}) collective-permute-start(f32[2,128,256]{2,1,0:T(8,128)S(1)} %get-tuple-element.65), channel_id=1, source_target_pairs={{0,9},{1,8},{2,11},{3,10},{4,13},{5,12},{6,15},{7,14},{8,1},{9,0},... | collective-permute-start | bytes 786440 | tf_op jit(solution)/shard_map/ppermute | solution.py:422
  89.0 49.4 %collective-permute-start.2 = (f32[2,128,256]{2,1,0:T(8,128)}, f32[2,128,256]{2,1,0:T(8,128)S(1)}, u32[]{:S(2)}, u32[]{:S(2)}) collective-permute-start(f32[2,128,256]{2,1,0:T(8,128)} %get-tuple-element.66), channel_id=1, source_target_pairs={{0,10},{1,11},{2,8},{3,9},{4,14},{5,15},{6,12},{7,13},{8,2},{9,3},... | collective-permute-start | bytes 786440 | tf_op jit(solution)/shard_map/ppermute | solution.py:422
  91.3 50.7 %collective-permute-start.3 = (f32[2,128,256]{2,1,0:T(8,128)}, f32[2,128,256]{2,1,0:T(8,128)S(1)}, u32[]{:S(2)}, u32[]{:S(2)}) collective-permute-start(f32[2,128,256]{2,1,0:T(8,128)} %get-tuple-element.67), channel_id=1, source_target_pairs={{0,11},{1,10},{2,9},{3,8},{4,15},{5,14},{6,13},{7,12},{8,3},{9,2},... | collective-permute-start | bytes 786440 | tf_op jit(solution)/shard_map/ppermute | solution.py:422
  92.5 49.6 %collective-permute-start.4 = (f32[2,128,256]{2,1,0:T(8,128)}, f32[2,128,256]{2,1,0:T(8,128)}, u32[]{:S(2)}, u32[]{:S(2)}) collective-permute-start(f32[2,128,256]{2,1,0:T(8,128)} %get-tuple-element.68), channel_id=1, source_target_pairs={{0,12},{1,13},{2,14},{3,15},{4,8},{5,9},{6,10},{7,11},{8,4},{9,5},... | collective-permute-start | bytes 786440 | tf_op jit(solution)/shard_map/ppermute | solution.py:422
  124.4 54.9 %collective-permute-start.27 = (f32[2,128,256]{2,1,0:T(8,128)}, f32[2,128,256]{2,1,0:T(8,128)}, u32[]{:S(2)}, u32[]{:S(2)}) collective-permute-start(f32[2,128,256]{2,1,0:T(8,128)} %get-tuple-element.114), channel_id=1, source_target_pairs={{0,13},{1,12},{2,15},{3,14},{4,9},{5,8},{6,11},{7,10},{8,5},{9,4},... | collective-permute-start | bytes 786440 | tf_op jit(solution)/shard_map/ppermute | solution.py:422
  131.0 50.1 %collective-permute-start.28 = (f32[2,128,256]{2,1,0:T(8,128)}, f32[2,128,256]{2,1,0:T(8,128)}, u32[]{:S(2)}, u32[]{:S(2)}) collective-permute-start(f32[2,128,256]{2,1,0:T(8,128)} %get-tuple-element.115), channel_id=1, source_target_pairs={{0,14},{1,15},{2,12},{3,13},{4,10},{5,11},{6,8},{7,9},{8,6},{9,7},... | collective-permute-start | bytes 786440 | tf_op jit(solution)/shard_map/ppermute | solution.py:422
  158.6 22.5 %collective-permute-start.12 = (f32[2,128,256]{2,1,0:T(8,128)S(1)}, f32[2,128,256]{2,1,0:T(8,128)S(1)}, u32[]{:S(2)}, u32[]{:S(2)}) collective-permute-start(f32[2,128,256]{2,1,0:T(8,128)S(1)} %get-tuple-element.88), channel_id=1, source_target_pairs={{0,8},{1,9},{2,10},{3,11},{4,12},{5,13},{6,14},{7,15},{8,0},{9,1},... | collective-permute-start | bytes 786440 | tf_op jit(solution)/shard_map/ppermute | solution.py:422
  163.7 38.8 %collective-permute-start.13 = (f32[2,128,256]{2,1,0:T(8,128)S(1)}, f32[2,128,256]{2,1,0:T(8,128)S(1)}, u32[]{:S(2)}, u32[]{:S(2)}) collective-permute-start(f32[2,128,256]{2,1,0:T(8,128)S(1)} %get-tuple-element.89), channel_id=1, source_target_pairs={{0,9},{1,8},{2,11},{3,10},{4,13},{5,12},{6,15},{7,14},{8,1},{9,0},... | collective-permute-start | bytes 786440 | tf_op jit(solution)/shard_map/ppermute | solution.py:422
  176.7 33.4 %collective-permute-start.14 = (f32[2,128,256]{2,1,0:T(8,128)S(1)}, f32[2,128,256]{2,1,0:T(8,128)S(1)}, u32[]{:S(2)}, u32[]{:S(2)}) collective-permute-start(f32[2,128,256]{2,1,0:T(8,128)S(1)} %get-tuple-element.90), channel_id=1, source_target_pairs={{0,10},{1,11},{2,8},{3,9},{4,14},{5,15},{6,12},{7,13},{8,2},{9,3},... | collective-permute-start | bytes 786440 | tf_op jit(solution)/shard_map/ppermute | solution.py:422
  179.3 38.4 %collective-permute-start.29 = (f32[2,128,256]{2,1,0:T(8,128)}, f32[2,128,256]{2,1,0:T(8,128)S(1)}, u32[]{:S(2)}, u32[]{:S(2)}) collective-permute-start(f32[2,128,256]{2,1,0:T(8,128)} %get-tuple-element.116), channel_id=1, source_target_pairs={{0,15},{1,14},{2,13},{3,12},{4,11},{5,10},{6,9},{7,8},{8,7},{9,6},... | collective-permute-start | bytes 786440 | tf_op jit(solution)/shard_map/ppermute | solution.py:422
  181.1 36.6 %collective-permute-start.5 = (f32[2,128,256]{2,1,0:T(8,128)}, f32[2,128,256]{2,1,0:T(8,128)S(1)}, u32[]{:S(2)}, u32[]{:S(2)}) collective-permute-start(f32[2,128,256]{2,1,0:T(8,128)} %get-tuple-element.73), channel_id=1, source_target_pairs={{0,1},{1,0},{2,3},{3,2},{4,5},{5,4},{6,7},{7,6},{8,9},{9,8},{10,11... | collective-permute-start | bytes 786440 | tf_op jit(solution)/shard_map/ppermute | solution.py:422
  181.1 38.8 %collective-permute-start.6 = (f32[2,128,256]{2,1,0:T(8,128)}, f32[2,128,256]{2,1,0:T(8,128)S(1)}, u32[]{:S(2)}, u32[]{:S(2)}) collective-permute-start(f32[2,128,256]{2,1,0:T(8,128)} %get-tuple-element.74), channel_id=1, source_target_pairs={{0,2},{1,3},{2,0},{3,1},{4,6},{5,7},{6,4},{7,5},{8,10},{9,11},{10,... | collective-permute-start | bytes 786440 | tf_op jit(solution)/shard_map/ppermute | solution.py:422
  221.8 19.7 %collective-permute-start.21 = (f32[2,128,256]{2,1,0:T(8,128)}, f32[2,128,256]{2,1,0:T(8,128)}, u32[]{:S(2)}, u32[]{:S(2)}) collective-permute-start(f32[2,128,256]{2,1,0:T(8,128)} %copy-done.12), channel_id=1, source_target_pairs={{0,2},{1,3},{2,0},{3,1},{4,6},{5,7},{6,4},{7,5},{8,10},{9,11},{10,... | collective-permute-start | bytes 786440 | tf_op jit(solution)/shard_map/ppermute | solution.py:422
  227.0 20.3 %collective-permute-start.22 = (f32[2,128,256]{2,1,0:T(8,128)}, f32[2,128,256]{2,1,0:T(8,128)}, u32[]{:S(2)}, u32[]{:S(2)}) collective-permute-start(f32[2,128,256]{2,1,0:T(8,128)} %copy-done.6), channel_id=1, source_target_pairs={{0,3},{1,2},{2,1},{3,0},{4,7},{5,6},{6,5},{7,4},{8,11},{9,10},{10,... | collective-permute-start | bytes 786440 | tf_op jit(solution)/shard_map/ppermute | solution.py:422
  238.8 20.5 %collective-permute-start.25 = (f32[2,128,256]{2,1,0:T(8,128)}, f32[2,128,256]{2,1,0:T(8,128)}, u32[]{:S(2)}, u32[]{:S(2)}) collective-permute-start(f32[2,128,256]{2,1,0:T(8,128)} %copy-done.3), channel_id=1, source_target_pairs={{0,6},{1,7},{2,4},{3,5},{4,2},{5,3},{6,0},{7,1},{8,14},{9,15},{10,... | collective-permute-start | bytes 786440 | tf_op jit(solution)/shard_map/ppermute | solution.py:422
  241.5 21.9 %collective-permute-start.26 = (f32[2,128,256]{2,1,0:T(8,128)S(1)}, f32[2,128,256]{2,1,0:T(8,128)}, u32[]{:S(2)}, u32[]{:S(2)}) collective-permute-start(f32[2,128,256]{2,1,0:T(8,128)S(1)} %get-tuple-element.108), channel_id=1, source_target_pairs={{0,7},{1,6},{2,5},{3,4},{4,3},{5,2},{6,1},{7,0},{8,15},{9,14},{10,... | collective-permute-start | bytes 786440 | tf_op jit(solution)/shard_map/ppermute | solution.py:422
  247.3 34.3 %collective-permute-start.15 = (f32[2,128,256]{2,1,0:T(8,128)}, f32[2,128,256]{2,1,0:T(8,128)S(1)}, u32[]{:S(2)}, u32[]{:S(2)}) collective-permute-start(f32[2,128,256]{2,1,0:T(8,128)} %copy-done.11), channel_id=1, source_target_pairs={{0,11},{1,10},{2,9},{3,8},{4,15},{5,14},{6,13},{7,12},{8,3},{9,2},... | collective-permute-start | bytes 786440 | tf_op jit(solution)/shard_map/ppermute | solution.py:422
  249.9 36.6 %collective-permute-start.16 = (f32[2,128,256]{2,1,0:T(8,128)}, f32[2,128,256]{2,1,0:T(8,128)S(1)}, u32[]{:S(2)}, u32[]{:S(2)}) collective-permute-start(f32[2,128,256]{2,1,0:T(8,128)} %copy-done.10), channel_id=1, source_target_pairs={{0,12},{1,13},{2,14},{3,15},{4,8},{5,9},{6,10},{7,11},{8,4},{9,5},... | collective-permute-start | bytes 786440 | tf_op jit(solution)/shard_map/ppermute | solution.py:422
  249.9 46.3 %collective-permute-start.17 = (f32[2,128,256]{2,1,0:T(8,128)}, f32[2,128,256]{2,1,0:T(8,128)S(1)}, u32[]{:S(2)}, u32[]{:S(2)}) collective-permute-start(f32[2,128,256]{2,1,0:T(8,128)} %copy-done.9), channel_id=1, source_target_pairs={{0,13},{1,12},{2,15},{3,14},{4,9},{5,8},{6,11},{7,10},{8,5},{9,4},... | collective-permute-start | bytes 786440 | tf_op jit(solution)/shard_map/ppermute | solution.py:422
  259.3 42.9 %collective-permute-start.18 = (f32[2,128,256]{2,1,0:T(8,128)}, f32[2,128,256]{2,1,0:T(8,128)S(1)}, u32[]{:S(2)}, u32[]{:S(2)}) collective-permute-start(f32[2,128,256]{2,1,0:T(8,128)} %copy-done.8), channel_id=1, source_target_pairs={{0,14},{1,15},{2,12},{3,13},{4,10},{5,11},{6,8},{7,9},{8,6},{9,7},... | collective-permute-start | bytes 786440 | tf_op jit(solution)/shard_map/ppermute | solution.py:422
  263.4 44.5 %collective-permute-start.19 = (f32[2,128,256]{2,1,0:T(8,128)}, f32[2,128,256]{2,1,0:T(8,128)S(1)}, u32[]{:S(2)}, u32[]{:S(2)}) collective-permute-start(f32[2,128,256]{2,1,0:T(8,128)} %copy-done.7), channel_id=1, source_target_pairs={{0,15},{1,14},{2,13},{3,12},{4,11},{5,10},{6,9},{7,8},{8,7},{9,6},... | collective-permute-start | bytes 786440 | tf_op jit(solution)/shard_map/ppermute | solution.py:422
  (46 other events, 508.6 us)

commit v2 on v1

--- a/solution.py
+++ b/solution.py
@@ -14,8 +14,8 @@
 EDGE = 64
 TILE = 256
 CHUNKS = [2, 2]
-HELD = 5
-KEPT = 3
+HELD = 4
+KEPT = 2
 CROSS = True
 STEP = 128
 UNROLL = 4

time: 327 us -> 321 us (0.982)
    all_to_all x2, waiting for transfers between devices: 39.2 us -> 33.2 us  [shards(): lax.all_to_all(sent, 'ang', 0, 0, axis_index_groups=groups, tiled=True)]
    ppermute x30, waiting for transfers between devices: 114 us -> 118 us  [deliver(): return lax.ppermute(part, 'ang', pairs)]
  transfers between devices with their start and end apart: 32 -> 32, of which waited for: 17 -> 20; matrix products, arithmetic and copies ran while one was open for 2% -> 2% of each run, Pallas kernels for 13% -> 14%
where the time goes in v2:
time: 321 us; the launch traced here: 320 us
  waiting for transfers between devices  151 us (47%)
  starting transfers between devices  75.1 us (23%)
  Pallas kernels  69.3 us (22%)
  local copies, waits for them, and re-layouts  18.9 us (6%)
    ppermute x30, waiting for transfers between devices, deliver(): return lax.ppermute(part, 'ang', pairs)  118 us
    ppermute x30, starting transfers between devices, deliver(): return lax.ppermute(part, 'ang', pairs)  63.2 us
    all_to_all x2, waiting for transfers between devices, shards(): lax.all_to_all(sent, 'ang', 0, 0, axis_index_groups=groups, tiled=True)  33.2 us
    pallas_call x2, Pallas kernels, ramp(): pl.pallas_call(functools.partial(ramp_kernel, total=total, parts=len(part...  29.5 us
    pallas_call x2, Pallas kernels, prepare(): pl.pallas_call(functools.partial(prepare_kernel, start=start), out_shape=...  19.6 us
    pallas_call x2, Pallas kernels, destripe(): pl.pallas_call(destripe_kernel, out_shape=shapes, grid_spec=pltpu.Prefetc...  17.4 us
    unnamed x82, local copies, waits for them, and re-layouts  16.8 us
    all_to_all x2, starting transfers between devices, shards(): lax.all_to_all(sent, 'ang', 0, 0, axis_index_groups=groups, tiled=True)  11.8 us
  transfers between devices with their start and end apart: 32, of which 20 were waited for; matrix products, arithmetic and copies ran while one was open for 2% of the time, Pallas kernels for 14%

profile of v2, /device:TPU:15, one launch (start us, length us, event | category | flops | bytes accessed | tf_op | source)
XLA Modules:
  0.0 319.9 jit_solution(9351413736181117445)
XLA Ops:
  2.6 9.8 %prepare.3 = f32[8,2,256,256]{3,2,1,0:T(8,128)} custom-call(s32[2]{0:T(128)} %pad_add_fusion.1.scalars, s32[256]{0:T(256)} %dark_index.3, s32[256]{0:T(256)} %flat_index.3, f32[16384,128]{1,0:T(8,128)} %bitcast.48, f32[4,64,128]{2,1,0:T(8,128)} %bitcast.52, f32[8,64,128]{2,1,0:T(8,128)} %bitcast.50, f32[1,2048]{1,0:T(1,128)} %broadcast_select_fusion.weight_ref), custom_call_target="tpu_custom_call" | custom-call | flops 20971520 | bytes 12582912 | tf_op jit(solution)/shard_map/prepare/pallas_call | solution.py:177
  12.5 5.4 %all-to-all-start.1 = ((f32[8,2,256,256]{3,2,1,0:T(8,128)}), f32[8,2,256,256]{3,2,1,0:T(8,128)}, u32[]{:S(2)}, u32[]{:S(2)}) async-start(f32[8,2,256,256]{3,2,1,0:T(8,128)} %prepare.3), calls=%async_computation.1 | async-start | bytes 8388608 | tf_op jit(solution)/shard_map/all_to_all | solution.py:431
  22.5 9.8 %prepare.2 = f32[8,2,256,256]{3,2,1,0:T(8,128)} custom-call(s32[2]{0:T(128)} %pad_add_fusion.1.scalars, s32[256]{0:T(256)} %dark_index.3, s32[256]{0:T(256)} %flat_index.3, f32[16384,128]{1,0:T(8,128)} %bitcast.49, f32[4,64,128]{2,1,0:T(8,128)} %bitcast.53, f32[8,64,128]{2,1,0:T(8,128)} %bitcast.51, f32[1,2048]{1,0:T(1,128)} %broadcast_select_fusion.weight_ref), custom_call_target="tpu_custom_call" | custom-call | flops 20971520 | bytes 12582912 | tf_op jit(solution)/shard_map/prepare/pallas_call | solution.py:177
  32.3 31.9 %all-to-all-done.1.x_ref = f32[8,2,256,256]{3,2,1,0:T(8,128)} async-done(((f32[8,2,256,256]{3,2,1,0:T(8,128)}), f32[8,2,256,256]{3,2,1,0:T(8,128)}, u32[]{:S(2)}, u32[]{:S(2)}) %all-to-all-start.1) | async-done | bytes 4194336 | tf_op jit(solution)/shard_map/all_to_all | solution.py:431
  64.1 6.5 %all-to-all-start = ((f32[8,2,256,256]{3,2,1,0:T(8,128)}), f32[8,2,256,256]{3,2,1,0:T(8,128)}, u32[]{:S(2)}, u32[]{:S(2)}) async-start(f32[8,2,256,256]{3,2,1,0:T(8,128)} %prepare.2), calls=%async_computation | async-start | bytes 8388608 | tf_op jit(solution)/shard_map/all_to_all | solution.py:431
  72.4 8.7 %destripe.2 = (f32[2,128,256]{2,1,0:T(8,128)S(1)}, f32[2,128,256]{2,1,0:T(8,128)S(1)}, f32[2,128,256]{2,1,0:T(8,128)S(1)}, f32[2,128,256]{2,1,0:T(8,128)S(1)}, f...) custom-call(s32[2]{0:T(128)S(1)} %pad_add_fusion.scalars, ...), custom_call_target="tpu_custom_call" | custom-call | flops 4831838208 | bytes 12582912 | tf_op jit(solution)/shard_map/destripe/pallas_call | solution.py:258
  94.6 29.8 %collective-permute-done.refs_8_ = f32[2,128,256]{2,1,0:T(8,128)S(1)} collective-permute-done((f32[2,128,256]{2,1,0:T(8,128)S(1)}, f32[2,128,256]{2,1,0:T(8,128)S(1)}, u32[]{:S(2)}, u32[]{:S(2)}) %collective-permute-start) | collective-permute-done | bytes 262176 | tf_op jit(solution)/shard_map/ppermute | solution.py:422
  124.9 6.1 %collective-permute-done.1.refs_9_ = f32[2,128,256]{2,1,0:T(8,128)S(1)} collective-permute-done((f32[2,128,256]{2,1,0:T(8,128)S(1)}, f32[2,128,256]{2,1,0:T(8,128)S(1)}, u32[]{:S(2)}, u32[]{:S(2)}) %collective-permute-start.1) | collective-permute-done | bytes 262176 | tf_op jit(solution)/shard_map/ppermute | solution.py:422
  131.0 4.7 %collective-permute-done.2.refs_10_ = f32[2,128,256]{2,1,0:T(8,128)S(1)} collective-permute-done((f32[2,128,256]{2,1,0:T(8,128)S(1)}, f32[2,128,256]{2,1,0:T(8,128)S(1)}, u32[]{:S(2)}, u32[]{:S(2)}) %collective-permute-start.2) | collective-permute-done | bytes 262176 | tf_op jit(solution)/shard_map/ppermute | solution.py:422
  143.6 8.7 %destripe.3 = (f32[2,128,256]{2,1,0:T(8,128)S(1)}, f32[2,128,256]{2,1,0:T(8,128)}, f32[2,128,256]{2,1,0:T(8,128)}, f32[2,128,256]{2,1,0:T(8,128)}, f32[2,128,256...) custom-call(s32[2]{0:T(128)S(1)} %pad_add_fusion.scalars, ...), custom_call_target="tpu_custom_call" | custom-call | flops 4831838208 | bytes 12582912 | tf_op jit(solution)/shard_map/destripe/pallas_call | solution.py:258
  158.6 22.6 %collective-permute-start.12 = (f32[2,128,256]{2,1,0:T(8,128)S(1)}, f32[2,128,256]{2,1,0:T(8,128)S(1)}, u32[]{:S(2)}, u32[]{:S(2)}) collective-permute-start(f32[2,128,256]{2,1,0:T(8,128)S(1)} %get-tuple-element.86), channel_id=1, source_target_pairs={{0,9},{1,8},{2,11},{3,10},{4,13},{5,12},{6,15},{7,14},{8,1},{9,0},... | collective-permute-start | bytes 786440 | tf_op jit(solution)/shard_map/ppermute | solution.py:422
  184.0 8.3 %collective-permute-done.29.refs_15_ = f32[2,128,256]{2,1,0:T(8,128)} collective-permute-done((f32[2,128,256]{2,1,0:T(8,128)}, f32[2,128,256]{2,1,0:T(8,128)}, u32[]{:S(2)}, u32[]{:S(2)}) %collective-permute-start.29) | collective-permute-done | bytes 262176 | tf_op jit(solution)/shard_map/ppermute | solution.py:422
  200.7 4.4 %collective-permute-start.8 = (f32[2,128,256]{2,1,0:T(8,128)}, f32[2,128,256]{2,1,0:T(8,128)S(1)}, u32[]{:S(2)}, u32[]{:S(2)}) collective-permute-start(f32[2,128,256]{2,1,0:T(8,128)} %get-tuple-element.74), channel_id=1, source_target_pairs={{0,5},{1,4},{2,7},{3,6},{4,1},{5,0},{6,3},{7,2},{8,13},{9,12},{10,... | collective-permute-start | bytes 786440 | tf_op jit(solution)/shard_map/ppermute | solution.py:422
  208.8 10.7 %collective-permute-done.8.refs_5_ = f32[2,128,256]{2,1,0:T(8,128)S(1)} collective-permute-done((f32[2,128,256]{2,1,0:T(8,128)}, f32[2,128,256]{2,1,0:T(8,128)S(1)}, u32[]{:S(2)}, u32[]{:S(2)}) %collective-permute-start.8) | collective-permute-done | bytes 262176 | tf_op jit(solution)/shard_map/ppermute | solution.py:422
  219.8 5.3 %collective-permute-done.9.refs_6_ = f32[2,128,256]{2,1,0:T(8,128)S(1)} collective-permute-done((f32[2,128,256]{2,1,0:T(8,128)}, f32[2,128,256]{2,1,0:T(8,128)S(1)}, u32[]{:S(2)}, u32[]{:S(2)}) %collective-permute-start.9) | collective-permute-done | bytes 262176 | tf_op jit(solution)/shard_map/ppermute | solution.py:422
  225.8 4.9 %collective-permute-done.10.refs_7_ = f32[2,128,256]{2,1,0:T(8,128)} collective-permute-done((f32[2,128,256]{2,1,0:T(8,128)}, f32[2,128,256]{2,1,0:T(8,128)}, u32[]{:S(2)}, u32[]{:S(2)}) %collective-permute-start.10) | collective-permute-done | bytes 262176 | tf_op jit(solution)/shard_map/ppermute | solution.py:422
  246.8 8.5 %collective-permute-done.24.refs_6_ = f32[2,128,256]{2,1,0:T(8,128)} collective-permute-done((f32[2,128,256]{2,1,0:T(8,128)}, f32[2,128,256]{2,1,0:T(8,128)}, u32[]{:S(2)}, u32[]{:S(2)}) %collective-permute-start.24) | collective-permute-done | bytes 262176 | tf_op jit(solution)/shard_map/ppermute | solution.py:422
  256.2 4.7 %collective-permute-done.25.refs_7_ = f32[2,128,256]{2,1,0:T(8,128)} collective-permute-done((f32[2,128,256]{2,1,0:T(8,128)S(1)}, f32[2,128,256]{2,1,0:T(8,128)}, u32[]{:S(2)}, u32[]{:S(2)}) %collective-permute-start.25) | collective-permute-done | bytes 262176 | tf_op jit(solution)/shard_map/ppermute | solution.py:422
  263.8 13.5 %ramp.2.refs_18_ = f32[2,128,4096]{2,1,0:T(8,128)S(1)} custom-call(s32[2]{0:T(128)S(1)} %pad_add_fusion.scalars, f32[2,128,256]{2,1,0:T(8,128)S(1)} %copy-done.18, f32[2,128,256]{2,1,0:T(8,128)} %collective-permute-done.19.refs_1_, f32[2,128,256]{2,1,0:T(8,128)} %collective-permute-done.20.refs_2_, f32[2,128,256]{2,1,0:T(8,128)} %collective-permute-done.21.refs_3_, ...), custom_call_target="tpu_custom_call" | custom-call | flops 9663676416 | bytes 16777216 | tf_op jit(solution)/shard_map/ramp/pallas_call | solution.py:354
  277.3 6.9 %collective-permute-done.15.refs_12_ = f32[2,128,256]{2,1,0:T(8,128)S(1)} collective-permute-done((f32[2,128,256]{2,1,0:T(8,128)}, f32[2,128,256]{2,1,0:T(8,128)S(1)}, u32[]{:S(2)}, u32[]{:S(2)}) %collective-permute-start.15) | collective-permute-done | bytes 262176 | tf_op jit(solution)/shard_map/ppermute | solution.py:422
  284.2 9.0 %collective-permute-done.16.refs_13_ = f32[2,128,256]{2,1,0:T(8,128)S(1)} collective-permute-done((f32[2,128,256]{2,1,0:T(8,128)}, f32[2,128,256]{2,1,0:T(8,128)S(1)}, u32[]{:S(2)}, u32[]{:S(2)}) %collective-permute-start.16) | collective-permute-done | bytes 262176 | tf_op jit(solution)/shard_map/ppermute | solution.py:422
  293.2 5.1 %collective-permute-done.17.refs_14_ = f32[2,128,256]{2,1,0:T(8,128)S(1)} collective-permute-done((f32[2,128,256]{2,1,0:T(8,128)}, f32[2,128,256]{2,1,0:T(8,128)S(1)}, u32[]{:S(2)}, u32[]{:S(2)}) %collective-permute-start.17) | collective-permute-done | bytes 262176 | tf_op jit(solution)/shard_map/ppermute | solution.py:422
  298.3 5.6 %collective-permute-done.18.refs_15_ = f32[2,128,256]{2,1,0:T(8,128)S(1)} collective-permute-done((f32[2,128,256]{2,1,0:T(8,128)}, f32[2,128,256]{2,1,0:T(8,128)S(1)}, u32[]{:S(2)}, u32[]{:S(2)}) %collective-permute-start.18) | collective-permute-done | bytes 262176 | tf_op jit(solution)/shard_map/ppermute | solution.py:422
  303.9 16.0 %ramp.3 = f32[128,128,128]{2,1,0:T(8,128)} custom-call(s32[2]{0:T(128)S(1)} %pad_add_fusion.scalars, f32[2,128,256]{2,1,0:T(8,128)S(1)} %copy-done.20, f32[2,128,256]{2,1,0:T(8,128)S(1)} %collective-permute-done.4.refs_1_, f32[2,128,256]{2,1,0:T(8,128)S(1)} %collective-permute-done.5.refs_2_, f32[2,128,256]{2,1,0:T(8,128)S(1)} %collective-permute-done.6.refs_3_, ...), custom_call_target="tpu_custom_call" | custom-call | flops 9663676416 | bytes 16777216 | tf_op jit(solution)/shard_map/ramp/pallas_call | solution.py:354
  (171 shorter events, 71.4 us)
Async XLA Ops:
  12.5 51.6 %all-to-all-start.1 = ((f32[8,2,256,256]{3,2,1,0:T(8,128)}), f32[8,2,256,256]{3,2,1,0:T(8,128)}, u32[]{:S(2)}, u32[]{:S(2)}) async-start(f32[8,2,256,256]{3,2,1,0:T(8,128)} %prepare.3), calls=%async_computation.1 | async-start | bytes 8388608 | tf_op jit(solution)/shard_map/all_to_all | solution.py:431
  64.1 74.3 %all-to-all-start = ((f32[8,2,256,256]{3,2,1,0:T(8,128)}), f32[8,2,256,256]{3,2,1,0:T(8,128)}, u32[]{:S(2)}, u32[]{:S(2)}) async-start(f32[8,2,256,256]{3,2,1,0:T(8,128)} %prepare.2), calls=%async_computation | async-start | bytes 8388608 | tf_op jit(solution)/shard_map/all_to_all | solution.py:431
  86.0 38.4 %collective-permute-start = (f32[2,128,256]{2,1,0:T(8,128)S(1)}, f32[2,128,256]{2,1,0:T(8,128)S(1)}, u32[]{:S(2)}, u32[]{:S(2)}) collective-permute-start(f32[2,128,256]{2,1,0:T(8,128)S(1)} %get-tuple-element.62), channel_id=1, source_target_pairs={{0,8},{1,9},{2,10},{3,11},{4,12},{5,13},{6,14},{7,15},{8,0},{9,1},... | collective-permute-start | bytes 786440 | tf_op jit(solution)/shard_map/ppermute | solution.py:422
  88.3 42.7 %collective-permute-start.1 = (f32[2,128,256]{2,1,0:T(8,128)S(1)}, f32[2,128,256]{2,1,0:T(8,128)S(1)}, u32[]{:S(2)}, u32[]{:S(2)}) collective-permute-start(f32[2,128,256]{2,1,0:T(8,128)S(1)} %get-tuple-element.63), channel_id=1, source_target_pairs={{0,9},{1,8},{2,11},{3,10},{4,13},{5,12},{6,15},{7,14},{8,1},{9,0},... | collective-permute-start | bytes 786440 | tf_op jit(solution)/shard_map/ppermute | solution.py:422
  88.9 46.8 %collective-permute-start.2 = (f32[2,128,256]{2,1,0:T(8,128)S(1)}, f32[2,128,256]{2,1,0:T(8,128)S(1)}, u32[]{:S(2)}, u32[]{:S(2)}) collective-permute-start(f32[2,128,256]{2,1,0:T(8,128)S(1)} %get-tuple-element.64), channel_id=1, source_target_pairs={{0,10},{1,11},{2,8},{3,9},{4,14},{5,15},{6,12},{7,13},{8,2},{9,3},... | collective-permute-start | bytes 786440 | tf_op jit(solution)/shard_map/ppermute | solution.py:422
  91.2 50.8 %collective-permute-start.3 = (f32[2,128,256]{2,1,0:T(8,128)}, f32[2,128,256]{2,1,0:T(8,128)S(1)}, u32[]{:S(2)}, u32[]{:S(2)}) collective-permute-start(f32[2,128,256]{2,1,0:T(8,128)} %get-tuple-element.65), channel_id=1, source_target_pairs={{0,11},{1,10},{2,9},{3,8},{4,15},{5,14},{6,13},{7,12},{8,3},{9,2},... | collective-permute-start | bytes 786440 | tf_op jit(solution)/shard_map/ppermute | solution.py:422
  93.3 65.3 %collective-permute-start.26 = (f32[2,128,256]{2,1,0:T(8,128)}, f32[2,128,256]{2,1,0:T(8,128)}, u32[]{:S(2)}, u32[]{:S(2)}) collective-permute-start(f32[2,128,256]{2,1,0:T(8,128)} %get-tuple-element.109), channel_id=1, source_target_pairs={{0,12},{1,13},{2,14},{3,15},{4,8},{5,9},{6,10},{7,11},{8,4},{9,5},... | collective-permute-start | bytes 786440 | tf_op jit(solution)/shard_map/ppermute | solution.py:422
  124.4 57.7 %collective-permute-start.27 = (f32[2,128,256]{2,1,0:T(8,128)}, f32[2,128,256]{2,1,0:T(8,128)}, u32[]{:S(2)}, u32[]{:S(2)}) collective-permute-start(f32[2,128,256]{2,1,0:T(8,128)} %get-tuple-element.110), channel_id=1, source_target_pairs={{0,13},{1,12},{2,15},{3,14},{4,9},{5,8},{6,11},{7,10},{8,5},{9,4},... | collective-permute-start | bytes 786440 | tf_op jit(solution)/shard_map/ppermute | solution.py:422
  131.0 52.9 %collective-permute-start.28 = (f32[2,128,256]{2,1,0:T(8,128)}, f32[2,128,256]{2,1,0:T(8,128)}, u32[]{:S(2)}, u32[]{:S(2)}) collective-permute-start(f32[2,128,256]{2,1,0:T(8,128)} %get-tuple-element.111), channel_id=1, source_target_pairs={{0,14},{1,15},{2,12},{3,13},{4,10},{5,11},{6,8},{7,9},{8,6},{9,7},... | collective-permute-start | bytes 786440 | tf_op jit(solution)/shard_map/ppermute | solution.py:422
  135.7 56.7 %collective-permute-start.29 = (f32[2,128,256]{2,1,0:T(8,128)}, f32[2,128,256]{2,1,0:T(8,128)}, u32[]{:S(2)}, u32[]{:S(2)}) collective-permute-start(f32[2,128,256]{2,1,0:T(8,128)} %get-tuple-element.112), channel_id=1, source_target_pairs={{0,15},{1,14},{2,13},{3,12},{4,11},{5,10},{6,9},{7,8},{8,7},{9,6},... | collective-permute-start | bytes 786440 | tf_op jit(solution)/shard_map/ppermute | solution.py:422
  158.6 36.5 %collective-permute-start.11 = (f32[2,128,256]{2,1,0:T(8,128)S(1)}, f32[2,128,256]{2,1,0:T(8,128)S(1)}, u32[]{:S(2)}, u32[]{:S(2)}) collective-permute-start(f32[2,128,256]{2,1,0:T(8,128)S(1)} %get-tuple-element.85), channel_id=1, source_target_pairs={{0,8},{1,9},{2,10},{3,11},{4,12},{5,13},{6,14},{7,15},{8,0},{9,1},... | collective-permute-start | bytes 786440 | tf_op jit(solution)/shard_map/ppermute | solution.py:422
  158.6 42.1 %collective-permute-start.12 = (f32[2,128,256]{2,1,0:T(8,128)S(1)}, f32[2,128,256]{2,1,0:T(8,128)S(1)}, u32[]{:S(2)}, u32[]{:S(2)}) collective-permute-start(f32[2,128,256]{2,1,0:T(8,128)S(1)} %get-tuple-element.86), channel_id=1, source_target_pairs={{0,9},{1,8},{2,11},{3,10},{4,13},{5,12},{6,15},{7,14},{8,1},{9,0},... | collective-permute-start | bytes 786440 | tf_op jit(solution)/shard_map/ppermute | solution.py:422
  182.1 23.4 %collective-permute-start.4 = (f32[2,128,256]{2,1,0:T(8,128)}, f32[2,128,256]{2,1,0:T(8,128)S(1)}, u32[]{:S(2)}, u32[]{:S(2)}) collective-permute-start(f32[2,128,256]{2,1,0:T(8,128)} %get-tuple-element.70), channel_id=1, source_target_pairs={{0,1},{1,0},{2,3},{3,2},{4,5},{5,4},{6,7},{7,6},{8,9},{9,8},{10,11... | collective-permute-start | bytes 786440 | tf_op jit(solution)/shard_map/ppermute | solution.py:422
  183.9 21.6 %collective-permute-start.5 = (f32[2,128,256]{2,1,0:T(8,128)}, f32[2,128,256]{2,1,0:T(8,128)S(1)}, u32[]{:S(2)}, u32[]{:S(2)}) collective-permute-start(f32[2,128,256]{2,1,0:T(8,128)} %get-tuple-element.71), channel_id=1, source_target_pairs={{0,2},{1,3},{2,0},{3,1},{4,6},{5,7},{6,4},{7,5},{8,10},{9,11},{10,... | collective-permute-start | bytes 786440 | tf_op jit(solution)/shard_map/ppermute | solution.py:422
  205.5 25.2 %collective-permute-start.10 = (f32[2,128,256]{2,1,0:T(8,128)}, f32[2,128,256]{2,1,0:T(8,128)}, u32[]{:S(2)}, u32[]{:S(2)}) collective-permute-start(f32[2,128,256]{2,1,0:T(8,128)} %copy-done.15), channel_id=1, source_target_pairs={{0,7},{1,6},{2,5},{3,4},{4,3},{5,2},{6,1},{7,0},{8,15},{9,14},{10,... | collective-permute-start | bytes 786440 | tf_op jit(solution)/shard_map/ppermute | solution.py:422
  208.0 24.9 %collective-permute-start.13 = (f32[2,128,256]{2,1,0:T(8,128)}, f32[2,128,256]{2,1,0:T(8,128)}, u32[]{:S(2)}, u32[]{:S(2)}) collective-permute-start(f32[2,128,256]{2,1,0:T(8,128)} %copy-done.14), channel_id=1, source_target_pairs={{0,10},{1,11},{2,8},{3,9},{4,14},{5,15},{6,12},{7,13},{8,2},{9,3},... | collective-permute-start | bytes 786440 | tf_op jit(solution)/shard_map/ppermute | solution.py:422
  208.2 25.1 %collective-permute-start.19 = (f32[2,128,256]{2,1,0:T(8,128)}, f32[2,128,256]{2,1,0:T(8,128)}, u32[]{:S(2)}, u32[]{:S(2)}) collective-permute-start(f32[2,128,256]{2,1,0:T(8,128)} %copy-done.13), channel_id=1, source_target_pairs={{0,1},{1,0},{2,3},{3,2},{4,5},{5,4},{6,7},{7,6},{8,9},{9,8},{10,11... | collective-permute-start | bytes 786440 | tf_op jit(solution)/shard_map/ppermute | solution.py:422
  233.3 22.0 %collective-permute-start.24 = (f32[2,128,256]{2,1,0:T(8,128)}, f32[2,128,256]{2,1,0:T(8,128)}, u32[]{:S(2)}, u32[]{:S(2)}) collective-permute-start(f32[2,128,256]{2,1,0:T(8,128)} %copy-done.3), channel_id=1, source_target_pairs={{0,6},{1,7},{2,4},{3,5},{4,2},{5,3},{6,0},{7,1},{8,14},{9,15},{10,... | collective-permute-start | bytes 786440 | tf_op jit(solution)/shard_map/ppermute | solution.py:422
  235.9 24.9 %collective-permute-start.25 = (f32[2,128,256]{2,1,0:T(8,128)S(1)}, f32[2,128,256]{2,1,0:T(8,128)}, u32[]{:S(2)}, u32[]{:S(2)}) collective-permute-start(f32[2,128,256]{2,1,0:T(8,128)S(1)} %get-tuple-element.104), channel_id=1, source_target_pairs={{0,7},{1,6},{2,5},{3,4},{4,3},{5,2},{6,1},{7,0},{8,15},{9,14},{10,... | collective-permute-start | bytes 786440 | tf_op jit(solution)/shard_map/ppermute | solution.py:422
  242.3 35.0 %collective-permute-start.14 = (f32[2,128,256]{2,1,0:T(8,128)}, f32[2,128,256]{2,1,0:T(8,128)S(1)}, u32[]{:S(2)}, u32[]{:S(2)}) collective-permute-start(f32[2,128,256]{2,1,0:T(8,128)} %copy-done.11), channel_id=1, source_target_pairs={{0,11},{1,10},{2,9},{3,8},{4,15},{5,14},{6,13},{7,12},{8,3},{9,2},... | collective-permute-start | bytes 786440 | tf_op jit(solution)/shard_map/ppermute | solution.py:422
  245.0 39.2 %collective-permute-start.15 = (f32[2,128,256]{2,1,0:T(8,128)}, f32[2,128,256]{2,1,0:T(8,128)S(1)}, u32[]{:S(2)}, u32[]{:S(2)}) collective-permute-start(f32[2,128,256]{2,1,0:T(8,128)} %copy-done.10), channel_id=1, source_target_pairs={{0,12},{1,13},{2,14},{3,15},{4,8},{5,9},{6,10},{7,11},{8,4},{9,5},... | collective-permute-start | bytes 786440 | tf_op jit(solution)/shard_map/ppermute | solution.py:422
  246.5 46.7 %collective-permute-start.16 = (f32[2,128,256]{2,1,0:T(8,128)}, f32[2,128,256]{2,1,0:T(8,128)S(1)}, u32[]{:S(2)}, u32[]{:S(2)}) collective-permute-start(f32[2,128,256]{2,1,0:T(8,128)} %copy-done.9), channel_id=1, source_target_pairs={{0,13},{1,12},{2,15},{3,14},{4,9},{5,8},{6,11},{7,10},{8,5},{9,4},... | collective-permute-start | bytes 786440 | tf_op jit(solution)/shard_map/ppermute | solution.py:422
  255.3 43.0 %collective-permute-start.17 = (f32[2,128,256]{2,1,0:T(8,128)}, f32[2,128,256]{2,1,0:T(8,128)S(1)}, u32[]{:S(2)}, u32[]{:S(2)}) collective-permute-start(f32[2,128,256]{2,1,0:T(8,128)} %copy-done.8), channel_id=1, source_target_pairs={{0,14},{1,15},{2,12},{3,13},{4,10},{5,11},{6,8},{7,9},{8,6},{9,7},... | collective-permute-start | bytes 786440 | tf_op jit(solution)/shard_map/ppermute | solution.py:422
  260.8 43.1 %collective-permute-start.18 = (f32[2,128,256]{2,1,0:T(8,128)}, f32[2,128,256]{2,1,0:T(8,128)S(1)}, u32[]{:S(2)}, u32[]{:S(2)}) collective-permute-start(f32[2,128,256]{2,1,0:T(8,128)} %copy-done.7), channel_id=1, source_target_pairs={{0,15},{1,14},{2,13},{3,12},{4,11},{5,10},{6,9},{7,8},{8,7},{9,6},... | collective-permute-start | bytes 786440 | tf_op jit(solution)/shard_map/ppermute | solution.py:422
  (46 other events, 522.1 us)

commit v3 on v2

--- a/solution.py
+++ b/solution.py
@@ -15,7 +15,7 @@
 TILE = 256
 CHUNKS = [2, 2]
 HELD = 4
-KEPT = 2
+KEPT = 1
 CROSS = True
 STEP = 128
 UNROLL = 4

time: 321 us -> 314 us (0.978)
  waiting for transfers between devices: 151 us -> 101 us
  starting transfers between devices: 75.1 us -> 117 us
    ppermute x30, waiting for transfers between devices: 118 us -> 67.7 us  [deliver(): return lax.ppermute(part, 'ang', pairs)]
    ppermute x30, starting transfers between devices: 63.2 us -> 105 us  [deliver(): return lax.ppermute(part, 'ang', pairs)]
  transfers between devices with their start and end apart: 32 -> 32, of which waited for: 20 -> 15; matrix products, arithmetic and copies ran while one was open for 2% -> 2% of each run, Pallas kernels for 14% -> 14%
where the time goes in v3:
time: 314 us; the launch traced here: 312 us
  starting transfers between devices  117 us (37%)
  waiting for transfers between devices  101 us (32%)
  Pallas kernels  69.3 us (22%)
  local copies, waits for them, and re-layouts  18.9 us (6%)
    ppermute x30, starting transfers between devices, deliver(): return lax.ppermute(part, 'ang', pairs)  105 us
    ppermute x30, waiting for transfers between devices, deliver(): return lax.ppermute(part, 'ang', pairs)  67.7 us
    all_to_all x2, waiting for transfers between devices, shards(): lax.all_to_all(sent, 'ang', 0, 0, axis_index_groups=groups, tiled=True)  33.2 us
    pallas_call x2, Pallas kernels, ramp(): pl.pallas_call(functools.partial(ramp_kernel, total=total, parts=len(part...  29.5 us
    pallas_call x2, Pallas kernels, prepare(): pl.pallas_call(functools.partial(prepare_kernel, start=start), out_shape=...  19.6 us
    pallas_call x2, Pallas kernels, destripe(): pl.pallas_call(destripe_kernel, out_shape=shapes, grid_spec=pltpu.Prefetc...  17.4 us
    unnamed x82, local copies, waits for them, and re-layouts  16.8 us
    all_to_all x2, starting transfers between devices, shards(): lax.all_to_all(sent, 'ang', 0, 0, axis_index_groups=groups, tiled=True)  11.8 us
  transfers between devices with their start and end apart: 32, of which 15 were waited for; matrix products, arithmetic and copies ran while one was open for 2% of the time, Pallas kernels for 14%

profile of v3, /device:TPU:15, one launch (start us, length us, event | category | flops | bytes accessed | tf_op | source)
XLA Modules:
  0.0 312.1 jit_solution(16637078801893694198)
XLA Ops:
  2.6 9.8 %prepare.3 = f32[8,2,256,256]{3,2,1,0:T(8,128)} custom-call(s32[2]{0:T(128)} %pad_add_fusion.1.scalars, s32[256]{0:T(256)} %dark_index.3, s32[256]{0:T(256)} %flat_index.3, f32[16384,128]{1,0:T(8,128)} %bitcast.48, f32[4,64,128]{2,1,0:T(8,128)} %bitcast.52, f32[8,64,128]{2,1,0:T(8,128)} %bitcast.50, f32[1,2048]{1,0:T(1,128)} %broadcast_select_fusion.weight_ref), custom_call_target="tpu_custom_call" | custom-call | flops 20971520 | bytes 12582912 | tf_op jit(solution)/shard_map/prepare/pallas_call | solution.py:177
  12.5 5.4 %all-to-all-start.1 = ((f32[8,2,256,256]{3,2,1,0:T(8,128)}), f32[8,2,256,256]{3,2,1,0:T(8,128)}, u32[]{:S(2)}, u32[]{:S(2)}) async-start(f32[8,2,256,256]{3,2,1,0:T(8,128)} %prepare.3), calls=%async_computation.1 | async-start | bytes 8388608 | tf_op jit(solution)/shard_map/all_to_all | solution.py:431
  22.5 9.8 %prepare.2 = f32[8,2,256,256]{3,2,1,0:T(8,128)} custom-call(s32[2]{0:T(128)} %pad_add_fusion.1.scalars, s32[256]{0:T(256)} %dark_index.3, s32[256]{0:T(256)} %flat_index.3, f32[16384,128]{1,0:T(8,128)} %bitcast.49, f32[4,64,128]{2,1,0:T(8,128)} %bitcast.53, f32[8,64,128]{2,1,0:T(8,128)} %bitcast.51, f32[1,2048]{1,0:T(1,128)} %broadcast_select_fusion.weight_ref), custom_call_target="tpu_custom_call" | custom-call | flops 20971520 | bytes 12582912 | tf_op jit(solution)/shard_map/prepare/pallas_call | solution.py:177
  32.3 31.9 %all-to-all-done.1.x_ref = f32[8,2,256,256]{3,2,1,0:T(8,128)} async-done(((f32[8,2,256,256]{3,2,1,0:T(8,128)}), f32[8,2,256,256]{3,2,1,0:T(8,128)}, u32[]{:S(2)}, u32[]{:S(2)}) %all-to-all-start.1) | async-done | bytes 4194336 | tf_op jit(solution)/shard_map/all_to_all | solution.py:431
  64.1 6.5 %all-to-all-start = ((f32[8,2,256,256]{3,2,1,0:T(8,128)}), f32[8,2,256,256]{3,2,1,0:T(8,128)}, u32[]{:S(2)}, u32[]{:S(2)}) async-start(f32[8,2,256,256]{3,2,1,0:T(8,128)} %prepare.2), calls=%async_computation | async-start | bytes 8388608 | tf_op jit(solution)/shard_map/all_to_all | solution.py:431
  72.4 8.7 %destripe.2 = (f32[2,128,256]{2,1,0:T(8,128)S(1)}, f32[2,128,256]{2,1,0:T(8,128)S(1)}, f32[2,128,256]{2,1,0:T(8,128)S(1)}, f32[2,128,256]{2,1,0:T(8,128)S(1)}, f...) custom-call(s32[2]{0:T(128)S(1)} %pad_add_fusion.scalars, ...), custom_call_target="tpu_custom_call" | custom-call | flops 4831838208 | bytes 12582912 | tf_op jit(solution)/shard_map/destripe/pallas_call | solution.py:258
  94.6 29.8 %collective-permute-done.refs_8_ = f32[2,128,256]{2,1,0:T(8,128)S(1)} collective-permute-done((f32[2,128,256]{2,1,0:T(8,128)S(1)}, f32[2,128,256]{2,1,0:T(8,128)S(1)}, u32[]{:S(2)}, u32[]{:S(2)}) %collective-permute-start) | collective-permute-done | bytes 262176 | tf_op jit(solution)/shard_map/ppermute | solution.py:422
  124.9 6.1 %collective-permute-done.1.refs_9_ = f32[2,128,256]{2,1,0:T(8,128)S(1)} collective-permute-done((f32[2,128,256]{2,1,0:T(8,128)S(1)}, f32[2,128,256]{2,1,0:T(8,128)S(1)}, u32[]{:S(2)}, u32[]{:S(2)}) %collective-permute-start.1) | collective-permute-done | bytes 262176 | tf_op jit(solution)/shard_map/ppermute | solution.py:422
  131.0 4.7 %collective-permute-done.2.refs_10_ = f32[2,128,256]{2,1,0:T(8,128)S(1)} collective-permute-done((f32[2,128,256]{2,1,0:T(8,128)S(1)}, f32[2,128,256]{2,1,0:T(8,128)S(1)}, u32[]{:S(2)}, u32[]{:S(2)}) %collective-permute-start.2) | collective-permute-done | bytes 262176 | tf_op jit(solution)/shard_map/ppermute | solution.py:422
  138.4 3.6 %collective-permute-done.3.refs_11_ = f32[2,128,256]{2,1,0:T(8,128)S(1)} collective-permute-done((f32[2,128,256]{2,1,0:T(8,128)}, f32[2,128,256]{2,1,0:T(8,128)S(1)}, u32[]{:S(2)}, u32[]{:S(2)}) %collective-permute-start.3) | collective-permute-done | bytes 262176 | tf_op jit(solution)/shard_map/ppermute | solution.py:422
  143.6 8.7 %destripe.3 = (f32[2,128,256]{2,1,0:T(8,128)S(1)}, f32[2,128,256]{2,1,0:T(8,128)S(1)}, f32[2,128,256]{2,1,0:T(8,128)}, f32[2,128,256]{2,1,0:T(8,128)}, f32[2,128...) custom-call(s32[2]{0:T(128)S(1)} %pad_add_fusion.scalars, ...), custom_call_target="tpu_custom_call" | custom-call | flops 4831838208 | bytes 12582912 | tf_op jit(solution)/shard_map/destripe/pallas_call | solution.py:258
  158.6 22.7 %collective-permute-start.11 = (f32[2,128,256]{2,1,0:T(8,128)S(1)}, f32[2,128,256]{2,1,0:T(8,128)S(1)}, u32[]{:S(2)}, u32[]{:S(2)}) collective-permute-start(f32[2,128,256]{2,1,0:T(8,128)S(1)} %get-tuple-element.84), channel_id=1, source_target_pairs={{0,8},{1,9},{2,10},{3,11},{4,12},{5,13},{6,14},{7,15},{8,0},{9,1},... | collective-permute-start | bytes 786440 | tf_op jit(solution)/shard_map/ppermute | solution.py:422
  184.2 3.1 collective-permute-start.8
  189.5 4.0 %collective-permute-start.9 = (f32[2,128,256]{2,1,0:T(8,128)}, f32[2,128,256]{2,1,0:T(8,128)S(1)}, u32[]{:S(2)}, u32[]{:S(2)}) collective-permute-start(f32[2,128,256]{2,1,0:T(8,128)} %get-tuple-element.74), channel_id=1, source_target_pairs={{0,6},{1,7},{2,4},{3,5},{4,2},{5,3},{6,0},{7,1},{8,14},{9,15},{10,... | collective-permute-start | bytes 786440 | tf_op jit(solution)/shard_map/ppermute | solution.py:422
  200.0 13.7 %collective-permute-start.19 = (f32[2,128,256]{2,1,0:T(8,128)}, f32[2,128,256]{2,1,0:T(8,128)}, u32[]{:S(2)}, u32[]{:S(2)}) collective-permute-start(f32[2,128,256]{2,1,0:T(8,128)} %copy-done.13), channel_id=1, source_target_pairs={{0,1},{1,0},{2,3},{3,2},{4,5},{5,4},{6,7},{7,6},{8,9},{9,8},{10,11... | collective-permute-start | bytes 786440 | tf_op jit(solution)/shard_map/ppermute | solution.py:422
  215.9 5.2 %collective-permute-done.10.refs_7_ = f32[2,128,256]{2,1,0:T(8,128)S(1)} collective-permute-done((f32[2,128,256]{2,1,0:T(8,128)}, f32[2,128,256]{2,1,0:T(8,128)S(1)}, u32[]{:S(2)}, u32[]{:S(2)}) %collective-permute-start.10) | collective-permute-done | bytes 262176 | tf_op jit(solution)/shard_map/ppermute | solution.py:422
  229.2 2.6 collective-permute-start.25
  235.3 4.0 %collective-permute-start.14 = (f32[2,128,256]{2,1,0:T(8,128)}, f32[2,128,256]{2,1,0:T(8,128)S(1)}, u32[]{:S(2)}, u32[]{:S(2)}) collective-permute-start(f32[2,128,256]{2,1,0:T(8,128)} %copy-done.11), channel_id=1, source_target_pairs={{0,11},{1,10},{2,9},{3,8},{4,15},{5,14},{6,13},{7,12},{8,3},{9,2},... | collective-permute-start | bytes 786440 | tf_op jit(solution)/shard_map/ppermute | solution.py:422
  241.7 4.3 %collective-permute-done.24.refs_6_ = f32[2,128,256]{2,1,0:T(8,128)} collective-permute-done((f32[2,128,256]{2,1,0:T(8,128)}, f32[2,128,256]{2,1,0:T(8,128)}, u32[]{:S(2)}, u32[]{:S(2)}) %collective-permute-start.24) | collective-permute-done | bytes 262176 | tf_op jit(solution)/shard_map/ppermute | solution.py:422
  246.0 5.7 %collective-permute-start.17 = (f32[2,128,256]{2,1,0:T(8,128)}, f32[2,128,256]{2,1,0:T(8,128)S(1)}, u32[]{:S(2)}, u32[]{:S(2)}) collective-permute-start(f32[2,128,256]{2,1,0:T(8,128)} %copy-done.8), channel_id=1, source_target_pairs={{0,14},{1,15},{2,12},{3,13},{4,10},{5,11},{6,8},{7,9},{8,6},{9,7},... | collective-permute-start | bytes 786440 | tf_op jit(solution)/shard_map/ppermute | solution.py:422
  251.7 25.9 %collective-permute-start.18 = (f32[2,128,256]{2,1,0:T(8,128)}, f32[2,128,256]{2,1,0:T(8,128)S(1)}, u32[]{:S(2)}, u32[]{:S(2)}) collective-permute-start(f32[2,128,256]{2,1,0:T(8,128)} %copy-done.7), channel_id=1, source_target_pairs={{0,15},{1,14},{2,13},{3,12},{4,11},{5,10},{6,9},{7,8},{8,7},{9,6},... | collective-permute-start | bytes 786440 | tf_op jit(solution)/shard_map/ppermute | solution.py:422
  278.5 13.5 %ramp.2.refs_18_ = f32[2,128,4096]{2,1,0:T(8,128)S(1)} custom-call(s32[2]{0:T(128)S(1)} %pad_add_fusion.scalars, f32[2,128,256]{2,1,0:T(8,128)S(1)} %copy-done.18, f32[2,128,256]{2,1,0:T(8,128)} %collective-permute-done.19.refs_1_, f32[2,128,256]{2,1,0:T(8,128)} %collective-permute-done.20.refs_2_, f32[2,128,256]{2,1,0:T(8,128)} %collective-permute-done.21.refs_3_, ...), custom_call_target="tpu_custom_call" | custom-call | flops 9663676416 | bytes 16777216 | tf_op jit(solution)/shard_map/ramp/pallas_call | solution.py:354
  292.0 4.1 %collective-permute-done.18.refs_15_ = f32[2,128,256]{2,1,0:T(8,128)S(1)} collective-permute-done((f32[2,128,256]{2,1,0:T(8,128)}, f32[2,128,256]{2,1,0:T(8,128)S(1)}, u32[]{:S(2)}, u32[]{:S(2)}) %collective-permute-start.18) | collective-permute-done | bytes 262176 | tf_op jit(solution)/shard_map/ppermute | solution.py:422
  296.1 16.0 %ramp.3 = f32[128,128,128]{2,1,0:T(8,128)} custom-call(s32[2]{0:T(128)S(1)} %pad_add_fusion.scalars, f32[2,128,256]{2,1,0:T(8,128)S(1)} %copy-done.20, f32[2,128,256]{2,1,0:T(8,128)S(1)} %collective-permute-done.4.refs_1_, f32[2,128,256]{2,1,0:T(8,128)S(1)} %collective-permute-done.5.refs_2_, f32[2,128,256]{2,1,0:T(8,128)S(1)} %collective-permute-done.6.refs_3_, ...), custom_call_target="tpu_custom_call" | custom-call | flops 9663676416 | bytes 16777216 | tf_op jit(solution)/shard_map/ramp/pallas_call | solution.py:354
  (171 shorter events, 60.8 us)
Async XLA Ops:
  12.5 51.6 %all-to-all-start.1 = ((f32[8,2,256,256]{3,2,1,0:T(8,128)}), f32[8,2,256,256]{3,2,1,0:T(8,128)}, u32[]{:S(2)}, u32[]{:S(2)}) async-start(f32[8,2,256,256]{3,2,1,0:T(8,128)} %prepare.3), calls=%async_computation.1 | async-start | bytes 8388608 | tf_op jit(solution)/shard_map/all_to_all | solution.py:431
  64.1 74.3 %all-to-all-start = ((f32[8,2,256,256]{3,2,1,0:T(8,128)}), f32[8,2,256,256]{3,2,1,0:T(8,128)}, u32[]{:S(2)}, u32[]{:S(2)}) async-start(f32[8,2,256,256]{3,2,1,0:T(8,128)} %prepare.2), calls=%async_computation | async-start | bytes 8388608 | tf_op jit(solution)/shard_map/all_to_all | solution.py:431
  86.0 38.4 %collective-permute-start = (f32[2,128,256]{2,1,0:T(8,128)S(1)}, f32[2,128,256]{2,1,0:T(8,128)S(1)}, u32[]{:S(2)}, u32[]{:S(2)}) collective-permute-start(f32[2,128,256]{2,1,0:T(8,128)S(1)} %get-tuple-element.61), channel_id=1, source_target_pairs={{0,8},{1,9},{2,10},{3,11},{4,12},{5,13},{6,14},{7,15},{8,0},{9,1},... | collective-permute-start | bytes 786440 | tf_op jit(solution)/shard_map/ppermute | solution.py:422
  88.3 42.7 %collective-permute-start.1 = (f32[2,128,256]{2,1,0:T(8,128)S(1)}, f32[2,128,256]{2,1,0:T(8,128)S(1)}, u32[]{:S(2)}, u32[]{:S(2)}) collective-permute-start(f32[2,128,256]{2,1,0:T(8,128)S(1)} %get-tuple-element.62), channel_id=1, source_target_pairs={{0,9},{1,8},{2,11},{3,10},{4,13},{5,12},{6,15},{7,14},{8,1},{9,0},... | collective-permute-start | bytes 786440 | tf_op jit(solution)/shard_map/ppermute | solution.py:422
  88.9 46.8 %collective-permute-start.2 = (f32[2,128,256]{2,1,0:T(8,128)S(1)}, f32[2,128,256]{2,1,0:T(8,128)S(1)}, u32[]{:S(2)}, u32[]{:S(2)}) collective-permute-start(f32[2,128,256]{2,1,0:T(8,128)S(1)} %get-tuple-element.63), channel_id=1, source_target_pairs={{0,10},{1,11},{2,8},{3,9},{4,14},{5,15},{6,12},{7,13},{8,2},{9,3},... | collective-permute-start | bytes 786440 | tf_op jit(solution)/shard_map/ppermute | solution.py:422
  91.2 50.8 %collective-permute-start.3 = (f32[2,128,256]{2,1,0:T(8,128)}, f32[2,128,256]{2,1,0:T(8,128)S(1)}, u32[]{:S(2)}, u32[]{:S(2)}) collective-permute-start(f32[2,128,256]{2,1,0:T(8,128)} %get-tuple-element.64), channel_id=1, source_target_pairs={{0,11},{1,10},{2,9},{3,8},{4,15},{5,14},{6,13},{7,12},{8,3},{9,2},... | collective-permute-start | bytes 786440 | tf_op jit(solution)/shard_map/ppermute | solution.py:422
  93.3 65.3 %collective-permute-start.26 = (f32[2,128,256]{2,1,0:T(8,128)}, f32[2,128,256]{2,1,0:T(8,128)}, u32[]{:S(2)}, u32[]{:S(2)}) collective-permute-start(f32[2,128,256]{2,1,0:T(8,128)} %get-tuple-element.107), channel_id=1, source_target_pairs={{0,12},{1,13},{2,14},{3,15},{4,8},{5,9},{6,10},{7,11},{8,4},{9,5},... | collective-permute-start | bytes 786440 | tf_op jit(solution)/shard_map/ppermute | solution.py:422
  124.4 57.7 %collective-permute-start.27 = (f32[2,128,256]{2,1,0:T(8,128)}, f32[2,128,256]{2,1,0:T(8,128)}, u32[]{:S(2)}, u32[]{:S(2)}) collective-permute-start(f32[2,128,256]{2,1,0:T(8,128)} %get-tuple-element.108), channel_id=1, source_target_pairs={{0,13},{1,12},{2,15},{3,14},{4,9},{5,8},{6,11},{7,10},{8,5},{9,4},... | collective-permute-start | bytes 786440 | tf_op jit(solution)/shard_map/ppermute | solution.py:422
  131.0 51.7 %collective-permute-start.28 = (f32[2,128,256]{2,1,0:T(8,128)}, f32[2,128,256]{2,1,0:T(8,128)}, u32[]{:S(2)}, u32[]{:S(2)}) collective-permute-start(f32[2,128,256]{2,1,0:T(8,128)} %get-tuple-element.109), channel_id=1, source_target_pairs={{0,14},{1,15},{2,12},{3,13},{4,10},{5,11},{6,8},{7,9},{8,6},{9,7},... | collective-permute-start | bytes 786440 | tf_op jit(solution)/shard_map/ppermute | solution.py:422
  135.7 48.5 %collective-permute-start.29 = (f32[2,128,256]{2,1,0:T(8,128)}, f32[2,128,256]{2,1,0:T(8,128)}, u32[]{:S(2)}, u32[]{:S(2)}) collective-permute-start(f32[2,128,256]{2,1,0:T(8,128)} %get-tuple-element.110), channel_id=1, source_target_pairs={{0,15},{1,14},{2,13},{3,12},{4,11},{5,10},{6,9},{7,8},{8,7},{9,6},... | collective-permute-start | bytes 786440 | tf_op jit(solution)/shard_map/ppermute | solution.py:422
  158.6 25.6 %collective-permute-start.4 = (f32[2,128,256]{2,1,0:T(8,128)S(1)}, f32[2,128,256]{2,1,0:T(8,128)S(1)}, u32[]{:S(2)}, u32[]{:S(2)}) collective-permute-start(f32[2,128,256]{2,1,0:T(8,128)S(1)} %get-tuple-element.69), channel_id=1, source_target_pairs={{0,1},{1,0},{2,3},{3,2},{4,5},{5,4},{6,7},{7,6},{8,9},{9,8},{10,11... | collective-permute-start | bytes 786440 | tf_op jit(solution)/shard_map/ppermute | solution.py:422
  158.6 30.9 %collective-permute-start.11 = (f32[2,128,256]{2,1,0:T(8,128)S(1)}, f32[2,128,256]{2,1,0:T(8,128)S(1)}, u32[]{:S(2)}, u32[]{:S(2)}) collective-permute-start(f32[2,128,256]{2,1,0:T(8,128)S(1)} %get-tuple-element.84), channel_id=1, source_target_pairs={{0,8},{1,9},{2,10},{3,11},{4,12},{5,13},{6,14},{7,15},{8,0},{9,1},... | collective-permute-start | bytes 786440 | tf_op jit(solution)/shard_map/ppermute | solution.py:422
  189.5 26.0 %collective-permute-start.9 = (f32[2,128,256]{2,1,0:T(8,128)}, f32[2,128,256]{2,1,0:T(8,128)S(1)}, u32[]{:S(2)}, u32[]{:S(2)}) collective-permute-start(f32[2,128,256]{2,1,0:T(8,128)} %get-tuple-element.74), channel_id=1, source_target_pairs={{0,6},{1,7},{2,4},{3,5},{4,2},{5,3},{6,0},{7,1},{8,14},{9,15},{10,... | collective-permute-start | bytes 786440 | tf_op jit(solution)/shard_map/ppermute | solution.py:422
  193.8 27.4 %collective-permute-start.10 = (f32[2,128,256]{2,1,0:T(8,128)}, f32[2,128,256]{2,1,0:T(8,128)S(1)}, u32[]{:S(2)}, u32[]{:S(2)}) collective-permute-start(f32[2,128,256]{2,1,0:T(8,128)} %copy-done.16), channel_id=1, source_target_pairs={{0,7},{1,6},{2,5},{3,4},{4,3},{5,2},{6,1},{7,0},{8,15},{9,14},{10,... | collective-permute-start | bytes 786440 | tf_op jit(solution)/shard_map/ppermute | solution.py:422
  196.3 27.1 %collective-permute-start.12 = (f32[2,128,256]{2,1,0:T(8,128)}, f32[2,128,256]{2,1,0:T(8,128)}, u32[]{:S(2)}, u32[]{:S(2)}) collective-permute-start(f32[2,128,256]{2,1,0:T(8,128)} %copy-done.15), channel_id=1, source_target_pairs={{0,9},{1,8},{2,11},{3,10},{4,13},{5,12},{6,15},{7,14},{8,1},{9,0},... | collective-permute-start | bytes 786440 | tf_op jit(solution)/shard_map/ppermute | solution.py:422
  196.3 28.4 %collective-permute-start.13 = (f32[2,128,256]{2,1,0:T(8,128)}, f32[2,128,256]{2,1,0:T(8,128)}, u32[]{:S(2)}, u32[]{:S(2)}) collective-permute-start(f32[2,128,256]{2,1,0:T(8,128)} %copy-done.14), channel_id=1, source_target_pairs={{0,10},{1,11},{2,8},{3,9},{4,14},{5,15},{6,12},{7,13},{8,2},{9,3},... | collective-permute-start | bytes 786440 | tf_op jit(solution)/shard_map/ppermute | solution.py:422
  200.0 26.2 %collective-permute-start.19 = (f32[2,128,256]{2,1,0:T(8,128)}, f32[2,128,256]{2,1,0:T(8,128)}, u32[]{:S(2)}, u32[]{:S(2)}) collective-permute-start(f32[2,128,256]{2,1,0:T(8,128)} %copy-done.13), channel_id=1, source_target_pairs={{0,1},{1,0},{2,3},{3,2},{4,5},{5,4},{6,7},{7,6},{8,9},{9,8},{10,11... | collective-permute-start | bytes 786440 | tf_op jit(solution)/shard_map/ppermute | solution.py:422
  226.2 19.7 %collective-permute-start.24 = (f32[2,128,256]{2,1,0:T(8,128)}, f32[2,128,256]{2,1,0:T(8,128)}, u32[]{:S(2)}, u32[]{:S(2)}) collective-permute-start(f32[2,128,256]{2,1,0:T(8,128)} %copy-done.3), channel_id=1, source_target_pairs={{0,6},{1,7},{2,4},{3,5},{4,2},{5,3},{6,0},{7,1},{8,14},{9,15},{10,... | collective-permute-start | bytes 786440 | tf_op jit(solution)/shard_map/ppermute | solution.py:422
  229.2 22.4 %collective-permute-start.25 = (f32[2,128,256]{2,1,0:T(8,128)S(1)}, f32[2,128,256]{2,1,0:T(8,128)}, u32[]{:S(2)}, u32[]{:S(2)}) collective-permute-start(f32[2,128,256]{2,1,0:T(8,128)S(1)} %get-tuple-element.102), channel_id=1, source_target_pairs={{0,7},{1,6},{2,5},{3,4},{4,3},{5,2},{6,1},{7,0},{8,15},{9,14},{10,... | collective-permute-start | bytes 786440 | tf_op jit(solution)/shard_map/ppermute | solution.py:422
  235.3 56.6 %collective-permute-start.14 = (f32[2,128,256]{2,1,0:T(8,128)}, f32[2,128,256]{2,1,0:T(8,128)S(1)}, u32[]{:S(2)}, u32[]{:S(2)}) collective-permute-start(f32[2,128,256]{2,1,0:T(8,128)} %copy-done.11), channel_id=1, source_target_pairs={{0,11},{1,10},{2,9},{3,8},{4,15},{5,14},{6,13},{7,12},{8,3},{9,2},... | collective-permute-start | bytes 786440 | tf_op jit(solution)/shard_map/ppermute | solution.py:422
  239.4 52.6 %collective-permute-start.15 = (f32[2,128,256]{2,1,0:T(8,128)}, f32[2,128,256]{2,1,0:T(8,128)S(1)}, u32[]{:S(2)}, u32[]{:S(2)}) collective-permute-start(f32[2,128,256]{2,1,0:T(8,128)} %copy-done.10), channel_id=1, source_target_pairs={{0,12},{1,13},{2,14},{3,15},{4,8},{5,9},{6,10},{7,11},{8,4},{9,5},... | collective-permute-start | bytes 786440 | tf_op jit(solution)/shard_map/ppermute | solution.py:422
  239.4 52.6 %collective-permute-start.16 = (f32[2,128,256]{2,1,0:T(8,128)}, f32[2,128,256]{2,1,0:T(8,128)S(1)}, u32[]{:S(2)}, u32[]{:S(2)}) collective-permute-start(f32[2,128,256]{2,1,0:T(8,128)} %copy-done.9), channel_id=1, source_target_pairs={{0,13},{1,12},{2,15},{3,14},{4,9},{5,8},{6,11},{7,10},{8,5},{9,4},... | collective-permute-start | bytes 786440 | tf_op jit(solution)/shard_map/ppermute | solution.py:422
  246.0 46.1 %collective-permute-start.17 = (f32[2,128,256]{2,1,0:T(8,128)}, f32[2,128,256]{2,1,0:T(8,128)S(1)}, u32[]{:S(2)}, u32[]{:S(2)}) collective-permute-start(f32[2,128,256]{2,1,0:T(8,128)} %copy-done.8), channel_id=1, source_target_pairs={{0,14},{1,15},{2,12},{3,13},{4,10},{5,11},{6,8},{7,9},{8,6},{9,7},... | collective-permute-start | bytes 786440 | tf_op jit(solution)/shard_map/ppermute | solution.py:422
  251.7 44.4 %collective-permute-start.18 = (f32[2,128,256]{2,1,0:T(8,128)}, f32[2,128,256]{2,1,0:T(8,128)S(1)}, u32[]{:S(2)}, u32[]{:S(2)}) collective-permute-start(f32[2,128,256]{2,1,0:T(8,128)} %copy-done.7), channel_id=1, source_target_pairs={{0,15},{1,14},{2,13},{3,12},{4,11},{5,10},{6,9},{7,8},{8,7},{9,6},... | collective-permute-start | bytes 786440 | tf_op jit(solution)/shard_map/ppermute | solution.py:422
  (46 other events, 483.1 us)
